TPU v7x, 32 devices: a whole 2x2x4 slice. The times are simulated.
32 devices in a mesh: groups: 2 (over x), seq: 16 (over z, y, core).
Axes of the slice: x: 2, y: 2, z: 4, core: 2. Of those that a mesh axis runs over, the one named last changes fastest.
Arguments:
- video_qkv: bfloat16 [4, 1536, 3, 4096], P('groups', 'seq'), parts along dimension 0, may hold values from -48 to 48
- video_cross_q: bfloat16 [4, 1536, 4096], P('groups', 'seq'), parts along dimension 0, may hold values from -48 to 48
- audio_kv_v: bfloat16 [4, 512, 2, 4096], P('groups', 'seq'), parts along dimension 0, may hold values from -4 to 4
- audio_qkv: bfloat16 [4, 512, 3, 2048], P('groups', 'seq'), parts along dimension 0, may hold values from -48 to 48
- audio_cross_q: bfloat16 [4, 512, 2048], P('groups', 'seq'), parts along dimension 0, may hold values from -48 to 48
- video_kv_a: bfloat16 [4, 1536, 2, 2048], P('groups', 'seq'), parts along dimension 0, may hold values from -4 to 4
- audio_valid: int32 [4], P('groups'), parts along dimension 0, may hold values from 256 to 512, as said below
- branch_prompt: int32 [4], P('groups'), parts along dimension 0, may hold values from 0 to 3
- video_gate: float32 [4, 4096], replicated, may hold values from 0.5 to 1.5
- audio_gate: float32 [4, 2048], replicated, may hold values from 0.5 to 1.5
Outputs:
- video_out: bfloat16 [4, 1536, 4096], P('groups', 'seq'), parts along dimension 0
- audio_out: bfloat16 [4, 512, 2048], P('groups', 'seq'), parts along dimension 0
There are 2 independent parts, one for each index of `groups`. A program takes and returns all parts, laid end to end along the dimension named above; an argument that names none is the same for every part. Nothing has to cross between parts.
Inputs may be any that keep to these rules, and one draw needn't show every extreme that they name: `audio_valid`: at least one branch has all 512 audio tokens valid.
All inputs are finite; a program needn't handle non-finite values.
Results may differ from a plain program's by a relative error of at most 0.0058.
Values may be sent and summed in bfloat16 or wider, within the bound.
A program may use at most 128 MiB of HBM per device.

v0:
```python
import jax
import jax.numpy as jnp
from jax import lax
from jax.sharding import PartitionSpec as P

HV = 32
HA = 16
PROMPTS = 4


def block_attend(queries, key_rows, value_rows, allowed):
    scores = jnp.dot(queries, key_rows.T, preferred_element_type=jnp.float32) * queries.shape[
        -1
    ] ** (-0.5)
    if allowed is not None:
        scores = jnp.where(allowed[None, :], scores, -jnp.inf)
    row_max = jnp.max(scores, axis=1, keepdims=True)
    weights = jnp.exp(scores - row_max)
    shares = (weights / jnp.sum(weights, axis=1, keepdims=True)).astype(jnp.bfloat16)
    return jnp.dot(shares, value_rows, preferred_element_type=jnp.float32).astype(jnp.bfloat16)


def attend(queries, key_rows, value_rows, allowed):
    row_count, head_width = queries.shape
    block_rows = row_count
    while block_rows % 2 == 0 and block_rows // 2 >= 512:
        block_rows = block_rows // 2

    def one_block(block_queries):
        return block_attend(block_queries, key_rows, value_rows, allowed)

    result = lax.map(one_block, queries.reshape(row_count // block_rows, block_rows, head_width))
    return result.reshape(row_count, head_width)


def to_items(source, head_count):
    lead_count, row_count = (source.shape[0], source.shape[1])
    middle = source.shape[2:-1]
    head_width = source.shape[-1] // head_count
    result = source.reshape((lead_count, row_count) + middle + (head_count, head_width))
    axes_order = (0, len(middle) + 2, 1) + tuple(range(2, len(middle) + 2)) + (len(middle) + 3,)
    result = jnp.transpose(result, axes_order)
    return result.reshape((lead_count * head_count, row_count) + middle + (head_width,))


def from_items(source, head_count):
    item_count, row_count, head_width = source.shape
    result = source.reshape(item_count // head_count, head_count, row_count, head_width)
    return jnp.transpose(result, (0, 2, 1, 3)).reshape(
        item_count // head_count, row_count, head_count * head_width
    )


def self_items(packed):
    return attend(packed[:, 0], packed[:, 1], packed[:, 2], None)


def self_masked(packed):
    return attend(packed[0][:, 0], packed[0][:, 1], packed[0][:, 2], packed[1] > 0.5)


def cross_masked(packed):
    return attend(packed[0], packed[1][:, 0], packed[1][:, 1], packed[2] > 0.5)


def cross_items(packed):
    return attend(packed[0], packed[1][:, 0], packed[1][:, 1], None)


def local_gates(gates, head_count, item_count):
    gate_items = to_items(gates[:, None, :], head_count)[:, 0, :]
    first_item = lax.axis_index("seq") * item_count
    return lax.dynamic_slice_in_dim(gate_items, first_item, item_count, 0)


def on_device(
    video_qkv,
    video_cross_q,
    audio_kv_v,
    audio_qkv,
    audio_cross_q,
    video_kv_a,
    audio_valid,
    branch_prompt,
    video_gate,
    audio_gate,
):
    local_audio = audio_qkv.shape[1]
    positions = lax.axis_index("seq") * local_audio + jnp.arange(local_audio, dtype=jnp.int32)
    allowed_local = (positions[None, :] < audio_valid[:, None]).astype(jnp.bfloat16)
    video_items = to_items(video_qkv, HV)
    video_query = to_items(video_cross_q, HV)
    video_keys = to_items(audio_kv_v, HV)
    video_allowed = jnp.repeat(allowed_local, HV, axis=0)
    audio_items = to_items(audio_qkv, HA)
    audio_query = to_items(audio_cross_q, HA)
    audio_keys = to_items(video_kv_a, HA)
    audio_allowed = jnp.repeat(allowed_local, HA, axis=0)
    video_items, video_query, video_keys, video_allowed = (
        lax.all_to_all(video_items, "seq", split_axis=0, concat_axis=1, tiled=True),
        lax.all_to_all(video_query, "seq", split_axis=0, concat_axis=1, tiled=True),
        lax.all_to_all(video_keys, "seq", split_axis=0, concat_axis=1, tiled=True),
        lax.all_to_all(video_allowed, "seq", split_axis=0, concat_axis=1, tiled=True),
    )
    audio_items, audio_query, audio_keys, audio_allowed = (
        lax.all_to_all(audio_items, "seq", split_axis=0, concat_axis=1, tiled=True),
        lax.all_to_all(audio_query, "seq", split_axis=0, concat_axis=1, tiled=True),
        lax.all_to_all(audio_keys, "seq", split_axis=0, concat_axis=1, tiled=True),
        lax.all_to_all(audio_allowed, "seq", split_axis=0, concat_axis=1, tiled=True),
    )
    video_self = lax.map(self_items, video_items)
    video_cross = lax.map(cross_masked, (video_query, video_keys, video_allowed))
    audio_self = lax.map(self_masked, (audio_items, audio_allowed))
    audio_cross = lax.map(cross_items, (audio_query, audio_keys))
    chosen = (branch_prompt[:, None] == jnp.arange(PROMPTS, dtype=jnp.int32)[None, :]).astype(
        jnp.float32
    )
    video_gates = jnp.dot(chosen, video_gate, precision=lax.Precision.HIGHEST)
    audio_gates = jnp.dot(chosen, audio_gate, precision=lax.Precision.HIGHEST)
    video_slice = local_gates(video_gates, HV, video_self.shape[0])
    audio_slice = local_gates(audio_gates, HA, audio_self.shape[0])
    video_return = (
        video_self.astype(jnp.float32) + video_slice[:, None, :] * video_cross.astype(jnp.float32)
    ).astype(jnp.bfloat16)
    audio_return = (
        audio_self.astype(jnp.float32) + audio_slice[:, None, :] * audio_cross.astype(jnp.float32)
    ).astype(jnp.bfloat16)
    video_back, audio_back = (
        lax.all_to_all(video_return, "seq", split_axis=1, concat_axis=0, tiled=True),
        lax.all_to_all(audio_return, "seq", split_axis=1, concat_axis=0, tiled=True),
    )
    return (from_items(video_back, HV), from_items(audio_back, HA))


def solution(mesh):
    placed = (
        P("groups", "seq", None, None),
        P("groups", "seq", None),
        P("groups", "seq", None, None),
        P("groups", "seq", None, None),
        P("groups", "seq", None),
        P("groups", "seq", None, None),
        P("groups"),
        P("groups"),
        P(),
        P(),
    )
    return jax.shard_map(
        on_device,
        mesh=mesh,
        in_specs=placed,
        out_specs=(P("groups", "seq", None), P("groups", "seq", None)),
        check_vma=False,
    )
```

profile of v0, /device:TPU:0, one launch (start us, length us, event | category | flops | bytes accessed | tf_op | source)
XLA Modules:
  0.0 376.8 jit_solution(1439106227688947911)
XLA Ops:
  2.1 7.4 %all-to-all-start.5 = ((bf16[16,2,32]{2,1,0:T(2,128)(2,1)}), bf16[16,2,32]{2,1,0:T(2,128)(2,1)S(1)}, u32[]{:S(2)}, u32[]{:S(2)}) async-start(bf16[16,2,32]{2,1,0:T(2,128)(2,1)} %broadcast_in_dim.90), calls=%async_computation.5 | async-start | bytes 16384 | tf_op jit(solution)/shard_map/all_to_all | solution.py:109
  9.5 1.0 copy.113
  10.5 5.3 %all-to-all-done.5 = bf16[16,2,32]{2,1,0:T(2,128)(2,1)S(1)} async-done(((bf16[16,2,32]{2,1,0:T(2,128)(2,1)}), bf16[16,2,32]{2,1,0:T(2,128)(2,1)S(1)}, u32[]{:S(2)}, u32[]{:S(2)}) %all-to-all-start.5) | async-done | bytes 2080 | tf_op jit(solution)/shard_map/all_to_all | solution.py:109
  16.4 3.5 all-to-all-start.3
  20.7 5.7 %all-to-all-done.3 = bf16[16,4,32]{2,1,0:T(4,128)(2,1)S(1)} async-done(((bf16[16,4,32]{2,1,0:T(4,128)(2,1)}), bf16[16,4,32]{2,1,0:T(4,128)(2,1)S(1)}, u32[]{:S(2)}, u32[]{:S(2)}) %all-to-all-start.3) | async-done | bytes 4128 | tf_op jit(solution)/shard_map/all_to_all | solution.py:103
  26.4 3.5 all-to-all-start.7
  30.1 1.1 copy.93
  31.2 8.7 %all-to-all-done.7 = bf16[32,32,128]{2,1,0:T(8,128)(2,1)S(1)} async-done(((bf16[32,32,128]{2,1,0:T(8,128)(2,1)}), bf16[32,32,128]{2,1,0:T(8,128)(2,1)S(1)}, u32[]{:S(2)}, u32[]{:S(2)}) %all-to-all-start.7) | async-done | bytes 262176 | tf_op jit(solution)/shard_map/all_to_all | solution.py:107
  40.6 3.6 all-to-all-start.6
  45.1 1.7 copy.85
  46.8 16.2 %all-to-all-done.6 = bf16[32,32,3,128]{3,1,2,0:T(8,128)(2,1)S(1)} async-done(((bf16[32,32,3,128]{3,1,2,0:T(8,128)(2,1)}), bf16[32,32,3,128]{3,1,2,0:T(8,128)(2,1)S(1)}, u32[]{:S(2)}, u32[]{:S(2)}) %all-to-all-start.6) | async-done | bytes 786464 | tf_op jit(solution)/shard_map/all_to_all | solution.py:106
  62.9 5.4 %all-to-all-start.2 = ((bf16[64,32,2,128]{3,1,2,0:T(8,128)(2,1)}), bf16[64,32,2,128]{3,1,2,0:T(8,128)(2,1)S(1)}, u32[]{:S(2)}, u32[]{:S(2)}) async-start(bf16[64,32,2,128]{3,1,2,0:T(8,128)(2,1)} %bitcast.36), calls=%async_computation.2 | async-start | bytes 2097152 | tf_op jit(solution)/shard_map/all_to_all | solution.py:102
  69.0 1.8 copy.82
  70.8 20.6 %all-to-all-done.2 = bf16[64,32,2,128]{3,1,2,0:T(8,128)(2,1)S(1)} async-done(((bf16[64,32,2,128]{3,1,2,0:T(8,128)(2,1)}), bf16[64,32,2,128]{3,1,2,0:T(8,128)(2,1)S(1)}, u32[]{:S(2)}, u32[]{:S(2)}) %all-to-all-start.2) | async-done | bytes 1048608 | tf_op jit(solution)/shard_map/all_to_all | solution.py:102
  91.3 1.0 copy-done.4
  92.3 6.9 %all-to-all-start.1 = ((bf16[64,96,128]{2,1,0:T(8,128)(2,1)}), bf16[64,96,128]{2,1,0:T(8,128)(2,1)S(1)}, u32[]{:S(2)}, u32[]{:S(2)}) async-start(bf16[64,96,128]{2,1,0:T(8,128)(2,1)} %bitcast.30), calls=%async_computation.1 | async-start | bytes 3145728 | tf_op jit(solution)/shard_map/all_to_all | solution.py:101
  99.2 2.8 reshape.114
  101.9 1.8 copy.98
  103.7 27.4 %all-to-all-done.1 = bf16[64,96,128]{2,1,0:T(8,128)(2,1)S(1)} async-done(((bf16[64,96,128]{2,1,0:T(8,128)(2,1)}), bf16[64,96,128]{2,1,0:T(8,128)(2,1)S(1)}, u32[]{:S(2)}, u32[]{:S(2)}) %all-to-all-start.1) | async-done | bytes 1572896 | tf_op jit(solution)/shard_map/all_to_all | solution.py:101
  131.1 1.1 copy-done.2
  132.3 9.2 %all-to-all-start.8 = ((bf16[32,96,2,128]{3,1,2,0:T(8,128)(2,1)}), bf16[32,96,2,128]{3,1,2,0:T(8,128)(2,1)}, u32[]{:S(2)}, u32[]{:S(2)}) async-start(bf16[32,96,2,128]{3,1,2,0:T(8,128)(2,1)} %bitcast.59), calls=%async_computation.8 | async-start | bytes 3145728 | tf_op jit(solution)/shard_map/all_to_all | solution.py:108
  141.4 3.8 %copy.110 = bf16[72,8,32,128]{3,2,1,0:T(8,128)(2,1)S(1)} copy(bf16[72,8,32,128]{3,1,2,0:T(8,128)(2,1)} %bitcast.241) | data formatting | bytes 9437184
  145.3 4.0 %copy.80 = bf16[2,32,96,3,128]{4,2,3,1,0:T(8,128)(2,1)} copy(bf16[2,32,96,3,128]{4,1,2,3,0:T(8,128)(2,1)S(1)} %bitcast.231) | data formatting | bytes 9437184 | tf_op jit(solution)/shard_map/transpose | solution.py:42
  150.8 2.1 while.72
  152.9 1.1 copy.86
  154.9 18.6 %all-to-all-done.8 = bf16[32,96,2,128]{3,1,2,0:T(8,128)(2,1)} async-done(((bf16[32,96,2,128]{3,1,2,0:T(8,128)(2,1)}), bf16[32,96,2,128]{3,1,2,0:T(8,128)(2,1)}, u32[]{:S(2)}, u32[]{:S(2)}) %all-to-all-start.8) | async-done | bytes 1572896 | tf_op jit(solution)/shard_map/all_to_all | solution.py:108
  173.5 9.2 %all-to-all-start = ((bf16[64,96,3,128]{3,1,2,0:T(8,128)(2,1)}), bf16[64,96,3,128]{3,1,2,0:T(8,128)(2,1)}, u32[]{:S(2)}, u32[]{:S(2)}) async-start(bf16[64,96,3,128]{3,1,2,0:T(8,128)(2,1)} %bitcast.230), calls=%async_computation | async-start | bytes 9437184 | tf_op jit(solution)/shard_map/all_to_all | solution.py:100
  182.6 1.5 copy.99
  184.9 6.3 %while.73 = (s32[]{:T(128)}, bf16[2,512,128]{2,1,0:T(8,128)(2,1)}, bf16[2,512,128]{2,1,0:T(8,128)(2,1)S(1)}, bf16[2,1536,2,128]{3,1,2,0:T(8,128)(2,1)S(1)}, s32[]{:T(128)}) while((s32[]{:T(128)}, bf16[2,512,128]{2,1,0:T(8,128)(2,1)}, bf16[2,512,128]{2,1,0:T(8,128)(2,1)S(1)}, bf16[2,1536,2,128]{3,1,2,0:T(8,128)(2,1)S(1)}, s32[]{:T(128)}) %tuple.140), condition=%wide.region_19.20_spmd, body=%wide.region_16.19_spmd.sunk | while | flops 408222720 | bytes 14166153 | solution.py:114
  191.2 1.1 add_convert_fusion.1
  193.3 1.3 broadcast.58.clone
  194.7 17.0 %while.71 = (s32[]{:T(128)}, bf16[4,1536,128]{2,1,0:T(8,128)(2,1)}, bf16[4,1536,128]{2,1,0:T(8,128)(2,1)S(1)}, bf16[4,512,2,128]{3,1,2,0:T(8,128)(2,1)}, bf16[4,...) while((s32[]{:T(128)}, bf16[4,1536,128]{2,1,0:T(8,128)(2,1)}, ...), condition=%wide.region_11.12_spmd, body=%wide.region_6.11_spmd.sunk | while | flops 204570624 | bytes 8015114 | solution.py:112
  194.7 1.0 dynamic-slice_bitcast_fusion.9
  195.7 2.4 while.75
  199.0 1.0 dynamic-slice_bitcast_fusion.9
  200.0 2.4 while.75
  204.2 2.4 while.75
  208.4 2.4 while.75
  211.6 57.8 %all-to-all-done = bf16[64,96,3,128]{3,1,2,0:T(8,128)(2,1)} async-done(((bf16[64,96,3,128]{3,1,2,0:T(8,128)(2,1)}), bf16[64,96,3,128]{3,1,2,0:T(8,128)(2,1)}, u32[]{:S(2)}, u32[]{:S(2)}) %all-to-all-start) | async-done | bytes 4718624 | tf_op jit(solution)/shard_map/all_to_all | solution.py:100
  269.4 21.8 %all-to-all-start.9 = ((bf16[2,512,128]{2,0,1:T(2,128)(2,1)}), bf16[2,512,128]{2,0,1:T(2,128)(2,1)}, u32[]{:S(2)}, u32[]{:S(2)}) async-start(bf16[2,512,128]{2,0,1:T(2,128)(2,1)} %copy.100), calls=%async_computation.9 | async-start | bytes 524288 | tf_op jit(solution)/shard_map/all_to_all | solution.py:130
  291.3 5.6 %copy.81 = bf16[4,16,96,3,128]{4,2,1,3,0:T(8,128)(2,1)} copy(bf16[4,16,96,3,128]{4,2,3,0,1:T(8,128)(2,1)} %bitcast.27) | data formatting | bytes 9437184 | tf_op jit(solution)/shard_map/all_to_all | solution.py:100
  297.1 29.7 %while.69 = (s32[]{:T(128)}, bf16[4,1536,128]{2,1,0:T(8,128)(2,1)S(1)}, bf16[4,1536,3,128]{3,1,2,0:T(8,128)(2,1)}, s32[]{:T(128)}, s32[]{:T(128)}, /*index=5*/s32[]{:T(128)}) while((s32[]{:T(128)}, bf16[4,1536,128]{2,1,0:T(8,128)(2,1)S(1)}, bf16[4,1536,3,128]{3,1,2,0:T(8,128)(2,1)}, s32[]{:T(128)}, s32[]{:T(128)}, /*index=5*/s32[]{:T(128)}) %tuple.136), condition=%wide.region_5.6_spmd, body=%wide.region_0.5_spmd.sunk | while | flops 614693376 | bytes 20858080 | solution.py:111
  297.1 1.4 dynamic-slice_bitcast_fusion.8
  298.5 5.9 %while.74 = (s32[]{:T(128)}, bf16[2,768,128]{2,1,0:T(8,128)(2,1)S(1)}, bf16[2,768,128]{2,1,0:T(8,128)(2,1)S(1)}, bf16[1536,128]{1,0:T(8,128)(2,1)S(1)}, bf16[1536,128]{1,0:T(8,128)(2,1)S(1)}, /*index=5*/s32[]{:T(128)}) while((s32[]{:T(128)}, bf16[2,768,128]{2,1,0:T(8,128)(2,1)S(1)}, bf16[2,768,128]{2,1,0:T(8,128)(2,1)S(1)}, ...), condition=%wide.region_4.4_spmd, body=%wide.region_1.3_spmd.sunk | while | flops 614693376 | bytes 15352917 | solution.py:32
  300.3 1.2 fusion.70
  303.2 1.2 fusion.70
  304.5 1.4 dynamic-slice_bitcast_fusion.8
  305.9 5.9 %while.74 = (s32[]{:T(128)}, bf16[2,768,128]{2,1,0:T(8,128)(2,1)S(1)}, bf16[2,768,128]{2,1,0:T(8,128)(2,1)S(1)}, bf16[1536,128]{1,0:T(8,128)(2,1)S(1)}, bf16[1536,128]{1,0:T(8,128)(2,1)S(1)}, /*index=5*/s32[]{:T(128)}) while((s32[]{:T(128)}, bf16[2,768,128]{2,1,0:T(8,128)(2,1)S(1)}, bf16[2,768,128]{2,1,0:T(8,128)(2,1)S(1)}, ...), condition=%wide.region_4.4_spmd, body=%wide.region_1.3_spmd.sunk | while | flops 614693376 | bytes 15352917 | solution.py:32
  307.7 1.2 fusion.70
  310.7 1.2 fusion.70
  311.9 1.4 dynamic-slice_bitcast_fusion.8
  313.4 5.9 %while.74 = (s32[]{:T(128)}, bf16[2,768,128]{2,1,0:T(8,128)(2,1)S(1)}, bf16[2,768,128]{2,1,0:T(8,128)(2,1)S(1)}, bf16[1536,128]{1,0:T(8,128)(2,1)S(1)}, bf16[1536,128]{1,0:T(8,128)(2,1)S(1)}, /*index=5*/s32[]{:T(128)}) while((s32[]{:T(128)}, bf16[2,768,128]{2,1,0:T(8,128)(2,1)S(1)}, bf16[2,768,128]{2,1,0:T(8,128)(2,1)S(1)}, ...), condition=%wide.region_4.4_spmd, body=%wide.region_1.3_spmd.sunk | while | flops 614693376 | bytes 15352917 | solution.py:32
  315.1 1.2 fusion.70
  318.1 1.2 fusion.70
  319.4 1.4 dynamic-slice_bitcast_fusion.8
  320.8 5.9 %while.74 = (s32[]{:T(128)}, bf16[2,768,128]{2,1,0:T(8,128)(2,1)S(1)}, bf16[2,768,128]{2,1,0:T(8,128)(2,1)S(1)}, bf16[1536,128]{1,0:T(8,128)(2,1)S(1)}, bf16[1536,128]{1,0:T(8,128)(2,1)S(1)}, /*index=5*/s32[]{:T(128)}) while((s32[]{:T(128)}, bf16[2,768,128]{2,1,0:T(8,128)(2,1)S(1)}, bf16[2,768,128]{2,1,0:T(8,128)(2,1)S(1)}, ...), condition=%wide.region_4.4_spmd, body=%wide.region_1.3_spmd.sunk | while | flops 614693376 | bytes 15352917 | solution.py:32
  322.6 1.2 fusion.70
  325.5 1.2 fusion.70
  326.8 1.9 add_convert_fusion
  328.7 8.2 %copy.88 = bf16[4,1536,128]{2,0,1:T(4,128)(2,1)} copy(bf16[4,1536,128]{2,1,0:T(8,128)(2,1)S(1)} %add_convert_fusion) | data formatting | bytes 3145728 | tf_op jit(solution)/shard_map/convert_element_type | solution.py:124
  336.9 6.0 %all-to-all-start.4 = ((bf16[4,1536,128]{2,0,1:T(4,128)(2,1)}), bf16[4,1536,128]{2,0,1:T(4,128)(2,1)S(1)}, u32[]{:S(2)}, u32[]{:S(2)}) async-start(bf16[4,1536,128]{2,0,1:T(4,128)(2,1)} %copy.88), calls=%async_computation.4 | async-start | bytes 3145728 | tf_op jit(solution)/shard_map/all_to_all | solution.py:129
  342.9 1.0 copy.101
  344.6 30.2 %all-to-all-done.4 = bf16[4,1536,128]{2,0,1:T(4,128)(2,1)S(1)} async-done(((bf16[4,1536,128]{2,0,1:T(4,128)(2,1)}), bf16[4,1536,128]{2,0,1:T(4,128)(2,1)S(1)}, u32[]{:S(2)}, u32[]{:S(2)}) %all-to-all-start.4) | async-done | bytes 1572896 | tf_op jit(solution)/shard_map/all_to_all | solution.py:129
  375.2 1.6 copy.116
  (165 shorter events, 48.1 us)
Async XLA Ops:
  0.6 148.6 %copy-start = (f32[4,4096]{1,0:T(4,128)S(1)}, f32[4,4096]{1,0:T(4,128)}, u32[]{:S(2)}) copy-start(f32[4,4096]{1,0:T(4,128)} %param.30) | copy-start | bytes 196612
  0.6 29.3 %copy-start.15 = (bf16[2,32,3,2048]{3,1,2,0:T(8,128)(2,1)S(1)}, bf16[2,32,3,2048]{3,1,2,0:T(8,128)(2,1)}, u32[]{:S(2)}) copy-start(bf16[2,32,3,2048]{3,1,2,0:T(8,128)(2,1)} %param.25) | copy-start | bytes 2359300
  2.1 13.7 %all-to-all-start.5 = ((bf16[16,2,32]{2,1,0:T(2,128)(2,1)}), bf16[16,2,32]{2,1,0:T(2,128)(2,1)S(1)}, u32[]{:S(2)}, u32[]{:S(2)}) async-start(bf16[16,2,32]{2,1,0:T(2,128)(2,1)} %broadcast_in_dim.90), calls=%async_computation.5 | async-start | bytes 16384 | tf_op jit(solution)/shard_map/all_to_all | solution.py:109
  16.4 10.0 %all-to-all-start.3 = ((bf16[16,4,32]{2,1,0:T(4,128)(2,1)}), bf16[16,4,32]{2,1,0:T(4,128)(2,1)S(1)}, u32[]{:S(2)}, u32[]{:S(2)}) async-start(bf16[16,4,32]{2,1,0:T(4,128)(2,1)} %broadcast_in_dim.89), calls=%async_computation.3 | async-start | bytes 32768 | tf_op jit(solution)/shard_map/all_to_all | solution.py:103
  26.4 13.5 %all-to-all-start.7 = ((bf16[32,32,128]{2,1,0:T(8,128)(2,1)}), bf16[32,32,128]{2,1,0:T(8,128)(2,1)S(1)}, u32[]{:S(2)}, u32[]{:S(2)}) async-start(bf16[32,32,128]{2,1,0:T(8,128)(2,1)} %bitcast.53), calls=%async_computation.7 | async-start | bytes 524288 | tf_op jit(solution)/shard_map/all_to_all | solution.py:107
  30.1 14.2 %copy-start.9 = (bf16[2,32,2,4096]{3,2,1,0:T(2,128)(2,1)S(1)}, bf16[2,32,2,4096]{3,2,1,0:T(2,128)(2,1)}, u32[]{:S(2)}) copy-start(bf16[2,32,2,4096]{3,2,1,0:T(2,128)(2,1)} %param.24) | copy-start | bytes 3145732
  39.9 0.7 copy-start.10
  40.6 22.3 %all-to-all-start.6 = ((bf16[32,32,3,128]{3,1,2,0:T(8,128)(2,1)}), bf16[32,32,3,128]{3,1,2,0:T(8,128)(2,1)S(1)}, u32[]{:S(2)}, u32[]{:S(2)}) async-start(bf16[32,32,3,128]{3,1,2,0:T(8,128)(2,1)} %bitcast.48), calls=%async_computation.6 | async-start | bytes 1572864 | tf_op jit(solution)/shard_map/all_to_all | solution.py:106
  46.8 21.6 %copy-start.8 = (bf16[2,96,4096]{2,1,0:T(8,128)(2,1)S(1)}, bf16[2,96,4096]{2,1,0:T(8,128)(2,1)}, u32[]{:S(2)}) copy-start(bf16[2,96,4096]{2,1,0:T(8,128)(2,1)} %param.23) | copy-start | bytes 4718596
  62.9 5.8 %copy-start.6 = (bf16[32,32,3,128]{3,1,2,0:T(8,128)(2,1)}, bf16[32,32,3,128]{3,1,2,0:T(8,128)(2,1)S(1)}, u32[]{:S(2)}) copy-start(bf16[32,32,3,128]{3,1,2,0:T(8,128)(2,1)S(1)} %all-to-all-done.6) | copy-start | bytes 2359300
  62.9 28.4 %all-to-all-start.2 = ((bf16[64,32,2,128]{3,1,2,0:T(8,128)(2,1)}), bf16[64,32,2,128]{3,1,2,0:T(8,128)(2,1)S(1)}, u32[]{:S(2)}, u32[]{:S(2)}) async-start(bf16[64,32,2,128]{3,1,2,0:T(8,128)(2,1)} %bitcast.36), calls=%async_computation.2 | async-start | bytes 2097152 | tf_op jit(solution)/shard_map/all_to_all | solution.py:102
  91.3 1.0 copy-start.4
  92.3 38.8 %all-to-all-start.1 = ((bf16[64,96,128]{2,1,0:T(8,128)(2,1)}), bf16[64,96,128]{2,1,0:T(8,128)(2,1)S(1)}, u32[]{:S(2)}, u32[]{:S(2)}) async-start(bf16[64,96,128]{2,1,0:T(8,128)(2,1)} %bitcast.30), calls=%async_computation.1 | async-start | bytes 3145728 | tf_op jit(solution)/shard_map/all_to_all | solution.py:101
  131.1 1.1 copy-start.2
  132.3 41.2 %all-to-all-start.8 = ((bf16[32,96,2,128]{3,1,2,0:T(8,128)(2,1)}), bf16[32,96,2,128]{3,1,2,0:T(8,128)(2,1)}, u32[]{:S(2)}, u32[]{:S(2)}) async-start(bf16[32,96,2,128]{3,1,2,0:T(8,128)(2,1)} %bitcast.59), calls=%async_computation.8 | async-start | bytes 3145728 | tf_op jit(solution)/shard_map/all_to_all | solution.py:108
  145.2 4.0 %copy-start.17 = (s32[2]{0:T(128)S(1)}, s32[2]{0:T(128)}, u32[]{:S(2)}) copy-start(s32[2]{0:T(128)} %param.29) | copy-start | bytes 28
  145.2 4.3 %copy-start.18 = (f32[4,2048]{1,0:T(4,128)S(1)}, f32[4,2048]{1,0:T(4,128)}, u32[]{:S(2)}) copy-start(f32[4,2048]{1,0:T(4,128)} %param.31) | copy-start | bytes 98308
  145.3 5.4 %copy-start.11 = (bf16[32,32,128]{2,1,0:T(8,128)(2,1)S(1)}, bf16[32,32,128]{2,1,0:T(8,128)(2,1)}, u32[]{:S(2)}) copy-start(bf16[32,32,128]{2,1,0:T(8,128)(2,1)} %copy-done.10) | copy-start | bytes 786436
  145.3 5.4 %copy-start.7 = (bf16[32,32,3,128]{3,1,2,0:T(8,128)(2,1)S(1)}, bf16[32,32,3,128]{3,1,2,0:T(8,128)(2,1)}, u32[]{:S(2)}) copy-start(bf16[32,32,3,128]{3,1,2,0:T(8,128)(2,1)} %copy-done.6) | copy-start | bytes 2359300
  150.8 2.1 copy-start.5
  152.9 2.0 copy-start.12
  152.9 1.9 copy-start.3
  173.5 96.0 %all-to-all-start = ((bf16[64,96,3,128]{3,1,2,0:T(8,128)(2,1)}), bf16[64,96,3,128]{3,1,2,0:T(8,128)(2,1)}, u32[]{:S(2)}, u32[]{:S(2)}) async-start(bf16[64,96,3,128]{3,1,2,0:T(8,128)(2,1)} %bitcast.230), calls=%async_computation | async-start | bytes 9437184 | tf_op jit(solution)/shard_map/all_to_all | solution.py:100
  185.7 1.0 copy-start.13
  187.4 0.7 copy-start.14
  188.8 1.0 copy-start.13
  190.5 0.7 copy-start.14
  269.4 67.5 %all-to-all-start.9 = ((bf16[2,512,128]{2,0,1:T(2,128)(2,1)}), bf16[2,512,128]{2,0,1:T(2,128)(2,1)}, u32[]{:S(2)}, u32[]{:S(2)}) async-start(bf16[2,512,128]{2,0,1:T(2,128)(2,1)} %copy.100), calls=%async_computation.9 | async-start | bytes 524288 | tf_op jit(solution)/shard_map/all_to_all | solution.py:130
  297.0 29.7 %copy-start.16 = (f32[4,128]{1,0:T(4,128)S(1)}, f32[4,128]{1,0:T(4,128)}, u32[]{:S(2)}) copy-start(f32[4,128]{1,0:T(4,128)} %constant_dynamic-slice_fusion.2) | copy-start | bytes 6148
  336.9 37.9 %all-to-all-start.4 = ((bf16[4,1536,128]{2,0,1:T(4,128)(2,1)}), bf16[4,1536,128]{2,0,1:T(4,128)(2,1)S(1)}, u32[]{:S(2)}, u32[]{:S(2)}) async-start(bf16[4,1536,128]{2,0,1:T(4,128)(2,1)} %copy.88), calls=%async_computation.4 | async-start | bytes 3145728 | tf_op jit(solution)/shard_map/all_to_all | solution.py:129
  375.2 1.6 copy-start.1
where the time goes:
time: 382 us; the launch traced here: 377 us
  waiting for transfers between devices  190 us (50%)
  starting transfers between devices  76.4 us (20%)
  local copies, waits for them, and re-layouts  65 us (17%)
  matrix products  28.3 us (7%)
  other arithmetic  14.8 us (4%)
    all_to_all x1, waiting for transfers between devices, on_device(): lax.all_to_all(video_items, 'seq', split_axis=0, concat_axis=1, tiled=True)  57.8 us
    all_to_all x1, waiting for transfers between devices, on_device(): lax.all_to_all(video_return, 'seq', split_axis=1, concat_axis=0, tiled=True)  30.2 us
    all_to_all x1, waiting for transfers between devices, on_device(): lax.all_to_all(video_query, 'seq', split_axis=0, concat_axis=1, tiled=True)  27.4 us
    all_to_all x1, starting transfers between devices, on_device(): lax.all_to_all(audio_return, 'seq', split_axis=1, concat_axis=0, tiled=True)  21.8 us
    all_to_all x1, waiting for transfers between devices, on_device(): lax.all_to_all(video_keys, 'seq', split_axis=0, concat_axis=1, tiled=True)  20.6 us
    all_to_all x1, waiting for transfers between devices, on_device(): lax.all_to_all(audio_keys, 'seq', split_axis=0, concat_axis=1, tiled=True)  18.6 us
    all_to_all x1, waiting for transfers between devices, on_device(): lax.all_to_all(audio_items, 'seq', split_axis=0, concat_axis=1, tiled=True)  16.2 us
    dot_general x20, matrix products, block_attend(): jnp.dot(shares, value_rows, preferred_element_type=jnp.float32)  16 us
  transfers between devices with their start and end apart: 10, of which 9 were waited for; matrix products, arithmetic and copies ran while one was open for 26% of the time, Pallas kernels for 0%

commit v1 on v0

v1 whole, which is shorter than its diff:
```python
import functools

import jax
import jax.numpy as jnp
from jax import lax
from jax.experimental import pallas as pl
from jax.experimental.pallas import tpu as pltpu
from jax.sharding import PartitionSpec as P

HV = 32
HA = 16
HEAD = 128
PROMPTS = 4
MESH = pl.DeviceIdType.MESH


def attend(queries, key_rows, value_rows, bias):
    scores = lax.dot_general(
        queries, key_rows, (((1,), (1,)), ((), ())), preferred_element_type=jnp.float32
    ) * (HEAD**-0.5)
    if bias is not None:
        scores = scores + bias
    row_max = jnp.max(scores, axis=1, keepdims=True)
    weights = jnp.exp(scores - row_max)
    total = jnp.sum(weights, axis=1, keepdims=True)
    result = jnp.dot(
        weights.astype(jnp.bfloat16), value_rows, preferred_element_type=jnp.float32
    )
    return (result / total).astype(jnp.bfloat16).astype(jnp.float32)


def block_kernel(
    n,
    video_count,
    audio_count,
    video_block,
    audio_block,
    video_qkv,
    video_q,
    audio_kv,
    audio_qkv,
    audio_q,
    video_kv,
    video_gates,
    audio_gates,
    bias,
    video_out,
    audio_out,
    video_qkv_in,
    video_q_in,
    audio_kv_in,
    audio_qkv_in,
    audio_q_in,
    video_kv_in,
    video_res,
    audio_res,
    video_sems,
    audio_sems,
    send_sems,
    back_sems,
):
    me = lax.axis_index("seq")
    group = lax.axis_index("groups")
    video_local = video_out.shape[1]
    audio_local = audio_out.shape[1]

    barrier = pltpu.get_barrier_semaphore()

    def greet(k, carry):
        peer = lax.rem(me + k, n)
        pl.semaphore_signal(barrier, inc=1, device_id=(group, peer), device_id_type=MESH)
        return carry

    lax.fori_loop(1, n, greet, 0)
    pl.semaphore_wait(barrier, n - 1)

    video_rows = pl.ds(pl.multiple_of(me * video_local, video_local), video_local)
    audio_rows = pl.ds(pl.multiple_of(me * audio_local, audio_local), audio_local)

    def columns(head):
        return pl.ds(pl.multiple_of(head * HEAD, HEAD), HEAD)

    def video_parts(item, slot):
        branch, head = item // HV, lax.rem(item, HV)
        return (
            (video_qkv.at[item], video_qkv_in.at[slot, :, video_rows], video_sems.at[slot, 0]),
            (
                video_q.at[branch, :, columns(head)],
                video_q_in.at[slot, video_rows],
                video_sems.at[slot, 1],
            ),
            (audio_kv.at[item], audio_kv_in.at[slot, :, audio_rows], video_sems.at[slot, 2]),
        )

    def audio_parts(item, slot):
        branch, head = item // HA, lax.rem(item, HA)
        return (
            (audio_qkv.at[item], audio_qkv_in.at[slot, :, audio_rows], audio_sems.at[slot, 0]),
            (
                audio_q.at[branch, :, columns(head)],
                audio_q_in.at[slot, audio_rows],
                audio_sems.at[slot, 1],
            ),
            (video_kv.at[item], video_kv_in.at[slot, :, video_rows], audio_sems.at[slot, 2]),
        )

    def send(parts, count, slot, first_sem):
        def to_peer(k, carry):
            peer = lax.rem(me + k, n)
            for place, (source, target, sem) in enumerate(parts(peer * count + slot, slot)):
                pltpu.make_async_remote_copy(
                    src_ref=source,
                    dst_ref=target,
                    send_sem=send_sems.at[first_sem + place],
                    recv_sem=sem,
                    device_id=(group, peer),
                    device_id_type=MESH,
                ).start()
            return carry

        lax.fori_loop(1, n, to_peer, 0)
        for source, target, sem in parts(me * count + slot, slot):
            pltpu.make_async_copy(source, target, sem).start()

    def send_video(slot, carry):
        send(video_parts, video_count, slot, 0)
        return carry

    def send_audio(slot, carry):
        send(audio_parts, audio_count, slot, 3)
        return carry

    lax.fori_loop(0, video_count, send_video, 0)
    lax.fori_loop(0, audio_count, send_audio, 0)

    def settle(ref, sem):
        pltpu.make_async_copy(ref, ref, sem).wait()

    def give_back(result, slot, out, branch, head, local, first, count, place):
        def to_peer(j, carry):
            peer = first + j
            source = result.at[slot, pl.ds(pl.multiple_of(peer * local, local), local)]
            target = out.at[branch, :, columns(head)]

            @pl.when(peer == me)
            def _():
                pltpu.make_async_copy(source, target, back_sems.at[place]).start()

            @pl.when(peer != me)
            def _():
                pltpu.make_async_remote_copy(
                    src_ref=source,
                    dst_ref=target,
                    send_sem=send_sems.at[6 + place],
                    recv_sem=back_sems.at[place],
                    device_id=(group, peer),
                    device_id_type=MESH,
                ).start()

            return carry

        lax.fori_loop(0, count, to_peer, 0)

    def video_item(slot, carry):
        item = me * video_count + slot
        branch, head = item // HV, lax.rem(item, HV)
        settle(video_qkv_in.at[slot], video_sems.at[slot, 0])
        settle(video_q_in.at[slot], video_sems.at[slot, 1])
        settle(audio_kv_in.at[slot], video_sems.at[slot, 2])
        block = video_block * video_local

        def rows(i, inner):
            here = pl.ds(pl.multiple_of(i * block, block), block)
            own = attend(
                video_qkv_in[slot, 0, here], video_qkv_in[slot, 1], video_qkv_in[slot, 2], None
            )
            cross = attend(
                video_q_in[slot, here], audio_kv_in[slot, 0], audio_kv_in[slot, 1], bias[branch]
            )
            video_res[slot, here] = (own + video_gates[item] * cross).astype(jnp.bfloat16)
            give_back(
                video_res, slot, video_out, branch, head, video_local, i * video_block,
                video_block, 0,
            )
            return inner

        lax.fori_loop(0, n // video_block, rows, 0)
        return carry

    def audio_item(slot, carry):
        item = me * audio_count + slot
        branch, head = item // HA, lax.rem(item, HA)
        settle(audio_qkv_in.at[slot], audio_sems.at[slot, 0])
        settle(audio_q_in.at[slot], audio_sems.at[slot, 1])
        settle(video_kv_in.at[slot], audio_sems.at[slot, 2])
        block = audio_block * audio_local

        def rows(i, inner):
            here = pl.ds(pl.multiple_of(i * block, block), block)
            own = attend(
                audio_qkv_in[slot, 0, here],
                audio_qkv_in[slot, 1],
                audio_qkv_in[slot, 2],
                bias[branch],
            )
            cross = attend(
                audio_q_in[slot, here], video_kv_in[slot, 0], video_kv_in[slot, 1], None
            )
            audio_res[slot, here] = (own + audio_gates[item] * cross).astype(jnp.bfloat16)
            give_back(
                audio_res, slot, audio_out, branch, head, audio_local, i * audio_block,
                audio_block, 1,
            )
            return inner

        lax.fori_loop(0, n // audio_block, rows, 0)
        return carry

    lax.fori_loop(0, video_count, video_item, 0)
    lax.fori_loop(0, audio_count, audio_item, 0)

    far_video = pl.ds(0, (n - 1) * video_local)
    far_audio = pl.ds(0, (n - 1) * audio_local)
    settle(video_qkv_in.at[:, :, far_video], send_sems.at[0])
    settle(video_q_in.at[:, far_video], send_sems.at[1])
    settle(audio_kv_in.at[:, :, far_audio], send_sems.at[2])
    settle(audio_qkv_in.at[:, :, far_audio], send_sems.at[3])
    settle(audio_q_in.at[:, far_audio], send_sems.at[4])
    settle(video_kv_in.at[:, :, far_video], send_sems.at[5])
    settle(video_res.at[:, far_video], send_sems.at[6])
    settle(audio_res.at[:, far_audio], send_sems.at[7])
    settle(video_out, back_sems.at[0])
    settle(audio_out, back_sems.at[1])


def by_items(source, head_count):
    branches, rows, kinds, width = source.shape
    result = source.reshape(branches, rows, kinds, head_count, width // head_count)
    return jnp.transpose(result, (0, 3, 2, 1, 4)).reshape(
        branches * head_count, kinds, rows, width // head_count
    )


def on_device(
    n,
    video_qkv,
    video_cross_q,
    audio_kv_v,
    audio_qkv,
    audio_cross_q,
    video_kv_a,
    audio_valid,
    branch_prompt,
    video_gate,
    audio_gate,
):
    branches, video_local = video_cross_q.shape[:2]
    audio_local = audio_cross_q.shape[1]
    video_all, audio_all = video_local * n, audio_local * n
    video_count, audio_count = branches * HV // n, branches * HA // n
    positions = jnp.arange(audio_all, dtype=jnp.int32)
    bias = jnp.where(positions[None, :] < audio_valid[:, None], 0.0, -jnp.inf).astype(jnp.float32)
    chosen = (branch_prompt[:, None] == jnp.arange(PROMPTS, dtype=jnp.int32)[None, :]).astype(
        jnp.float32
    )
    video_gates = jnp.dot(chosen, video_gate, precision=lax.Precision.HIGHEST)
    audio_gates = jnp.dot(chosen, audio_gate, precision=lax.Precision.HIGHEST)
    hbm = pl.BlockSpec(memory_space=pl.ANY)
    vmem = pl.BlockSpec(memory_space=pltpu.VMEM)
    half = jnp.bfloat16
    return tuple(
        pl.pallas_call(
            functools.partial(
                block_kernel, n, video_count, audio_count, min(4, n), min(8, n)
            ),
            out_shape=(
                jax.ShapeDtypeStruct(video_cross_q.shape, half),
                jax.ShapeDtypeStruct(audio_cross_q.shape, half),
            ),
            in_specs=[hbm] * 6 + [vmem] * 3,
            out_specs=(hbm, hbm),
            scratch_shapes=[
                pltpu.VMEM((video_count, 3, video_all, HEAD), half),
                pltpu.VMEM((video_count, video_all, HEAD), half),
                pltpu.VMEM((video_count, 2, audio_all, HEAD), half),
                pltpu.VMEM((audio_count, 3, audio_all, HEAD), half),
                pltpu.VMEM((audio_count, audio_all, HEAD), half),
                pltpu.VMEM((audio_count, 2, video_all, HEAD), half),
                pltpu.VMEM((video_count, video_all, HEAD), half),
                pltpu.VMEM((audio_count, audio_all, HEAD), half),
                pltpu.SemaphoreType.DMA((video_count, 3)),
                pltpu.SemaphoreType.DMA((audio_count, 3)),
                pltpu.SemaphoreType.DMA((8,)),
                pltpu.SemaphoreType.DMA((2,)),
            ],
            compiler_params=pltpu.CompilerParams(
                collective_id=0, has_side_effects=True, vmem_limit_bytes=48 * 2**20
            ),
        )(
            by_items(video_qkv, HV),
            video_cross_q,
            by_items(audio_kv_v, HV),
            by_items(audio_qkv, HA),
            audio_cross_q,
            by_items(video_kv_a, HA),
            video_gates.reshape(branches * HV, 1, HEAD),
            audio_gates.reshape(branches * HA, 1, HEAD),
            bias.reshape(branches, 1, audio_all),
        )
    )


def solution(mesh):
    placed = (
        P("groups", "seq", None, None),
        P("groups", "seq", None),
        P("groups", "seq", None, None),
        P("groups", "seq", None, None),
        P("groups", "seq", None),
        P("groups", "seq", None, None),
        P("groups"),
        P("groups"),
        P(),
        P(),
    )
    return jax.shard_map(
        functools.partial(on_device, mesh.shape["seq"]),
        mesh=mesh,
        in_specs=placed,
        out_specs=(P("groups", "seq", None), P("groups", "seq", None)),
        check_vma=False,
    )
```

time: 382 us -> 283 us (0.74); the launches traced: 377 us -> 283 us
  Pallas kernels: 0 us -> 260 us
  waiting for transfers between devices: 190 us -> 0 us
  starting transfers between devices: 76.4 us -> 0 us
  local copies, waits for them, and re-layouts: 65 us -> 18.9 us
  matrix products: 28.3 us -> 2.1 us
  other arithmetic: 14.8 us -> 0.8 us
    pallas_call x0 -> x1, Pallas kernels: none -> 260 us  [on_device(): pl.pallas_call(functools.partial(block_kernel, n, video_count, audio_coun...]
    all_to_all x10 -> x0, waiting for transfers between devices: 190 us -> none  [the longest x1 57.8 us: on_device(): lax.all_to_all(video_items, 'seq', split_axis=0, concat_axis=1, tiled=True)]
    all_to_all x10 -> x0, starting transfers between devices: 76.4 us -> none  [the longest x1 21.8 us: on_device(): lax.all_to_all(audio_return, 'seq', split_axis=1, concat_axis=0, tiled=True)]
    dot_general x40 -> x0, matrix products: 27.8 us -> none  [the longest x20 16 us: block_attend(): jnp.dot(shares, value_rows, preferred_element_type=jnp.float32)]
    transpose x8 -> x0, local copies, waits for them, and re-layouts: 11.3 us -> none  [to_items(): result = jnp.transpose(result, axes_order)]
    reshape x4 -> x8, local copies, waits for them, and re-layouts: 5.92 us -> 17.1 us  [the longest x6 17 us: by_items(): source.reshape(branches, rows, kinds, head_count, width // head_count)]
    reduce_sum x20 -> x0, other arithmetic: 10.8 us -> none  [block_attend(): jnp.sum(weights, axis=1, keepdims=True)]
    all_to_all x14 -> x0, local copies, waits for them, and re-layouts: 9.95 us -> none  [the longest x1 5.58 us: on_device(): lax.all_to_all(video_items, 'seq', split_axis=0, concat_axis=1, tiled=True)]
  transfers between devices with their start and end apart: 10 -> 0, of which waited for: 9 -> 0; matrix products, arithmetic and copies ran while one was open for 26% -> 0% of each run, Pallas kernels for 0% -> 0%
where the time goes in v1:
time: 283 us
  Pallas kernels  260 us (92%)
  local copies, waits for them, and re-layouts  18.9 us (7%)
    pallas_call x1, Pallas kernels, on_device(): pl.pallas_call(functools.partial(block_kernel, n, video_count, audio_coun...  260 us
    reshape x6, local copies, waits for them, and re-layouts, by_items(): source.reshape(branches, rows, kinds, head_count, width // head_count)  17 us

profile of v1, /device:TPU:0, one launch (start us, length us, event | category | flops | bytes accessed | tf_op | source)
XLA Modules:
  0.0 282.6 jit_solution(4265625640468886976)
XLA Ops:
  0.6 0.0 copy-start
  0.6 0.8 compare_select_fusion.bias
  1.4 1.0 fusion
  2.5 1.1 fusion.1
  3.6 0.1 reshape.74.video_gates
  3.7 0.0 copy-done
  3.7 0.1 copy_bitcast_fusion.1
  3.8 2.6 reshape.68
  6.5 1.9 copy.13
  8.4 3.7 %reshape.72 = bf16[2,96,2,16,128]{4,3,2,1,0:T(8,128)(2,1)} reshape(bf16[2,96,2,2048]{3,2,1,0:T(2,128)(2,1)} %param.15) | data formatting | bytes 3145728 | tf_op jit(solution)/shard_map/reshape | solution.py:238
  12.1 3.2 %copy.15 = bf16[2,96,2,16,128]{4,1,2,3,0:T(8,128)(2,1)} copy(bf16[2,96,2,16,128]{4,3,2,1,0:T(8,128)(2,1)} %reshape.72) | data formatting | bytes 3145728 | tf_op jit(solution)/shard_map/reshape | solution.py:238
  15.3 0.0 copy-start.1
  15.3 0.0 copy-start.2
  15.3 5.4 %copy_bitcast_fusion = bf16[2,96,3,32,128]{4,1,2,3,0:T(8,128)(2,1)} fusion(bf16[2,96,3,4096]{3,1,2,0:T(8,128)(2,1)} %param.10), kind=kLoop, calls=%fused_computation | loop fusion | bytes 9437184 | tf_op jit(solution)/shard_map/reshape | solution.py:238
  20.7 0.0 copy-done.1
  20.7 0.0 copy-done.2
  20.7 260.1 %shard_map.113 = (bf16[2,96,4096]{2,1,0:T(8,128)(2,1)S(1)}, bf16[2,32,2048]{2,1,0:T(8,128)(2,1)S(1)}) custom-call(bf16[64,3,96,128]{3,2,1,0:T(8,128)(2,1)} %bitcast.26, bf16[2,96,4096]{2,1,0:T(8,128)(2,1)S(1)} %copy-done.1, bf16[64,2,32,128]{3,2,1,0:T(8,128)(2,1)S(1)} %bitcast.24, bf16[32,3,32,128]{3,2,1,0:T(8,128)(2,1)S(1)} %bitcast.25, ...), custom_call_target="tpu_custom_call" | custom-call | tf_op jit(solution)/shard_map/pallas_call | solution.py:272
  280.8 1.1 copy.22
  281.9 0.7 copy.23
  (1 shorter events, 0.0 us)
Async XLA Ops:
  0.6 3.0 %copy-start = (bf16[2,32,3,2048]{3,1,2,0:T(8,128)(2,1)S(1)}, bf16[2,32,3,2048]{3,1,2,0:T(8,128)(2,1)}, u32[]{:S(2)}) copy-start(bf16[2,32,3,2048]{3,1,2,0:T(8,128)(2,1)} %param.13) | copy-start | bytes 2359300
  15.3 5.4 %copy-start.1 = (bf16[2,96,4096]{2,1,0:T(8,128)(2,1)S(1)}, bf16[2,96,4096]{2,1,0:T(8,128)(2,1)}, u32[]{:S(2)}) copy-start(bf16[2,96,4096]{2,1,0:T(8,128)(2,1)} %video_q.1) | copy-start | bytes 4718596
  15.3 5.4 %copy-start.2 = (bf16[2,32,2048]{2,1,0:T(8,128)(2,1)S(1)}, bf16[2,32,2048]{2,1,0:T(8,128)(2,1)}, u32[]{:S(2)}) copy-start(bf16[2,32,2048]{2,1,0:T(8,128)(2,1)} %audio_q.1) | copy-start | bytes 786436

commit v2 on v1

--- a/solution.py
+++ b/solution.py
@@ -32,6 +32,7 @@
 def block_kernel(
     n,
     video_count,
+    cross_count,
     audio_count,
     video_block,
     audio_block,
@@ -53,8 +54,12 @@
     audio_q_in,
     video_kv_in,
     video_res,
+    cross_res,
     audio_res,
+    own_home,
+    cross_home,
     video_sems,
+    cross_sems,
     audio_sems,
     send_sems,
     back_sems,
@@ -77,37 +82,71 @@
     video_rows = pl.ds(pl.multiple_of(me * video_local, video_local), video_local)
     audio_rows = pl.ds(pl.multiple_of(me * audio_local, audio_local), audio_local)
 
+    near = n // 2
+    half_first = (me // near) * near
+    place_in_half = me - half_first
+    half_rows = pl.ds(pl.multiple_of(place_in_half * video_local, video_local), video_local)
+
     def columns(head):
         return pl.ds(pl.multiple_of(head * HEAD, HEAD), HEAD)
 
     def video_parts(item, slot):
         branch, head = item // HV, lax.rem(item, HV)
         return (
-            (video_qkv.at[item], video_qkv_in.at[slot, :, video_rows], video_sems.at[slot, 0]),
+            (
+                video_qkv.at[branch, :, :, columns(head)],
+                video_qkv_in.at[slot, :, video_rows],
+                video_sems.at[slot],
+            ),
+        )
+
+    def cross_q_parts(item, slot):
+        branch, head = item // HV, lax.rem(item, HV)
+        return (
             (
                 video_q.at[branch, :, columns(head)],
-                video_q_in.at[slot, video_rows],
-                video_sems.at[slot, 1],
-            ),
-            (audio_kv.at[item], audio_kv_in.at[slot, :, audio_rows], video_sems.at[slot, 2]),
+                video_q_in.at[slot, half_rows],
+                cross_sems.at[slot, 0],
+            ),
+        )
+
+    def cross_kv_parts(item, slot):
+        branch, head = item // HV, lax.rem(item, HV)
+        return (
+            (
+                audio_kv.at[branch, :, :, columns(head)],
+                audio_kv_in.at[slot, :, audio_rows],
+                cross_sems.at[slot, 1],
+            ),
         )
 
     def audio_parts(item, slot):
         branch, head = item // HA, lax.rem(item, HA)
         return (
-            (audio_qkv.at[item], audio_qkv_in.at[slot, :, audio_rows], audio_sems.at[slot, 0]),
+            (
+                audio_qkv.at[branch, :, :, columns(head)],
+                audio_qkv_in.at[slot, :, audio_rows],
+                audio_sems.at[slot, 0],
+            ),
             (
                 audio_q.at[branch, :, columns(head)],
                 audio_q_in.at[slot, audio_rows],
                 audio_sems.at[slot, 1],
             ),
-            (video_kv.at[item], video_kv_in.at[slot, :, video_rows], audio_sems.at[slot, 2]),
+            (
+                video_kv.at[branch, :, :, columns(head)],
+                video_kv_in.at[slot, :, video_rows],
+                audio_sems.at[slot, 2],
+            ),
         )
 
-    def send(parts, count, slot, first_sem):
+    def send(parts, count, slot, first_sem, first, span, ring):
+        def items_of(peer):
+            return parts(lax.rem(peer, ring) * count + slot, slot)
+
         def to_peer(k, carry):
-            peer = lax.rem(me + k, n)
-            for place, (source, target, sem) in enumerate(parts(peer * count + slot, slot)):
+            peer = first + lax.rem(me - first + k, span)
+            for place, (source, target, sem) in enumerate(items_of(peer)):
                 pltpu.make_async_remote_copy(
                     src_ref=source,
                     dst_ref=target,
@@ -118,16 +157,25 @@
                 ).start()
             return carry
 
-        lax.fori_loop(1, n, to_peer, 0)
-        for source, target, sem in parts(me * count + slot, slot):
+        lax.fori_loop(1, span, to_peer, 0)
+        for source, target, sem in items_of(me):
             pltpu.make_async_copy(source, target, sem).start()
 
+    per_video = cross_count // video_count
+
     def send_video(slot, carry):
-        send(video_parts, video_count, slot, 0)
+        send(video_parts, video_count, slot, 0, 0, n, n)
+
+        def send_cross(j, inner):
+            send(cross_q_parts, cross_count, slot * per_video + j, 1, half_first, near, near)
+            send(cross_kv_parts, cross_count, slot * per_video + j, 2, 0, n, near)
+            return inner
+
+        lax.fori_loop(0, per_video, send_cross, 0)
         return carry
 
     def send_audio(slot, carry):
-        send(audio_parts, audio_count, slot, 3)
+        send(audio_parts, audio_count, slot, 3, 0, n, n)
         return carry
 
     lax.fori_loop(0, video_count, send_video, 0)
@@ -136,10 +184,10 @@
     def settle(ref, sem):
         pltpu.make_async_copy(ref, ref, sem).wait()
 
-    def give_back(result, slot, out, branch, head, local, first, count, place):
+    def give_back(result, slot, out, branch, head, local, base, first, count, place):
         def to_peer(j, carry):
-            peer = first + j
-            source = result.at[slot, pl.ds(pl.multiple_of(peer * local, local), local)]
+            peer = base + first + j
+            source = result.at[slot, pl.ds(pl.multiple_of((first + j) * local, local), local)]
             target = out.at[branch, :, columns(head)]
 
             @pl.when(peer == me)
@@ -164,9 +212,7 @@
     def video_item(slot, carry):
         item = me * video_count + slot
         branch, head = item // HV, lax.rem(item, HV)
-        settle(video_qkv_in.at[slot], video_sems.at[slot, 0])
-        settle(video_q_in.at[slot], video_sems.at[slot, 1])
-        settle(audio_kv_in.at[slot], video_sems.at[slot, 2])
+        settle(video_qkv_in.at[slot], video_sems.at[slot])
         block = video_block * video_local
 
         def rows(i, inner):
@@ -174,18 +220,42 @@
             own = attend(
                 video_qkv_in[slot, 0, here], video_qkv_in[slot, 1], video_qkv_in[slot, 2], None
             )
+            video_res[slot, here] = own.astype(jnp.bfloat16)
+            give_back(
+                video_res, slot, own_home, branch, head, video_local, 0, i * video_block,
+                video_block, 0,
+            )
+            return inner
+
+        lax.fori_loop(0, n // video_block, rows, 0)
+
+        def cross(j, inner):
+            cross_item(slot * per_video + j)
+            return inner
+
+        lax.fori_loop(0, per_video, cross, 0)
+        return carry
+
+    def cross_item(slot):
+        item = place_in_half * cross_count + slot
+        branch, head = item // HV, lax.rem(item, HV)
+        settle(video_q_in.at[slot], cross_sems.at[slot, 0])
+        settle(audio_kv_in.at[slot], cross_sems.at[slot, 1])
+        block = video_block * video_local
+
+        def rows(i, inner):
+            here = pl.ds(pl.multiple_of(i * block, block), block)
             cross = attend(
                 video_q_in[slot, here], audio_kv_in[slot, 0], audio_kv_in[slot, 1], bias[branch]
             )
-            video_res[slot, here] = (own + video_gates[item] * cross).astype(jnp.bfloat16)
+            cross_res[slot, here] = cross.astype(jnp.bfloat16)
             give_back(
-                video_res, slot, video_out, branch, head, video_local, i * video_block,
-                video_block, 0,
+                cross_res, slot, cross_home, branch, head, video_local, half_first,
+                i * video_block, video_block, 2,
             )
             return inner
 
-        lax.fori_loop(0, n // video_block, rows, 0)
-        return carry
+        lax.fori_loop(0, near // video_block, rows, 0)
 
     def audio_item(slot, carry):
         item = me * audio_count + slot
@@ -208,7 +278,7 @@
             )
             audio_res[slot, here] = (own + audio_gates[item] * cross).astype(jnp.bfloat16)
             give_back(
-                audio_res, slot, audio_out, branch, head, audio_local, i * audio_block,
+                audio_res, slot, audio_out, branch, head, audio_local, 0, i * audio_block,
                 audio_block, 1,
             )
             return inner
@@ -219,26 +289,38 @@
     lax.fori_loop(0, video_count, video_item, 0)
     lax.fori_loop(0, audio_count, audio_item, 0)
 
+    settle(own_home, back_sems.at[0])
+    settle(cross_home, back_sems.at[2])
+    width = 512
+
+    def combine(i, carry):
+        here = pl.ds(pl.multiple_of(i * width, width), width)
+        for branch in range(own_home.shape[0]):
+            video_out[branch, :, here] = (
+                own_home[branch, :, here].astype(jnp.float32)
+                + video_gates[branch, :, here] * cross_home[branch, :, here].astype(jnp.float32)
+            ).astype(jnp.bfloat16)
+        return carry
+
+    lax.fori_loop(0, video_out.shape[2] // width, combine, 0)
+
     far_video = pl.ds(0, (n - 1) * video_local)
     far_audio = pl.ds(0, (n - 1) * audio_local)
+    far_half = pl.ds(0, (near - 1) * video_local)
     settle(video_qkv_in.at[:, :, far_video], send_sems.at[0])
-    settle(video_q_in.at[:, far_video], send_sems.at[1])
+    settle(video_q_in.at[:, far_half], send_sems.at[1])
     settle(audio_kv_in.at[:, :, far_audio], send_sems.at[2])
     settle(audio_qkv_in.at[:, :, far_audio], send_sems.at[3])
     settle(audio_q_in.at[:, far_audio], send_sems.at[4])
     settle(video_kv_in.at[:, :, far_video], send_sems.at[5])
     settle(video_res.at[:, far_video], send_sems.at[6])
     settle(audio_res.at[:, far_audio], send_sems.at[7])
-    settle(video_out, back_sems.at[0])
+    settle(cross_res.at[:, far_half], send_sems.at[8])
     settle(audio_out, back_sems.at[1])
 
 
-def by_items(source, head_count):
-    branches, rows, kinds, width = source.shape
-    result = source.reshape(branches, rows, kinds, head_count, width // head_count)
-    return jnp.transpose(result, (0, 3, 2, 1, 4)).reshape(
-        branches * head_count, kinds, rows, width // head_count
-    )
+def kinds_first(source):
+    return jnp.transpose(source, (0, 2, 1, 3))
 
 
 def on_device(
@@ -258,6 +340,8 @@
     audio_local = audio_cross_q.shape[1]
     video_all, audio_all = video_local * n, audio_local * n
     video_count, audio_count = branches * HV // n, branches * HA // n
+    near = n // 2
+    cross_count = branches * HV // near
     positions = jnp.arange(audio_all, dtype=jnp.int32)
     bias = jnp.where(positions[None, :] < audio_valid[:, None], 0.0, -jnp.inf).astype(jnp.float32)
     chosen = (branch_prompt[:, None] == jnp.arange(PROMPTS, dtype=jnp.int32)[None, :]).astype(
@@ -271,39 +355,43 @@
     return tuple(
         pl.pallas_call(
             functools.partial(
-                block_kernel, n, video_count, audio_count, min(4, n), min(8, n)
+                block_kernel, n, video_count, cross_count, audio_count, min(4, near), min(8, n)
             ),
             out_shape=(
                 jax.ShapeDtypeStruct(video_cross_q.shape, half),
                 jax.ShapeDtypeStruct(audio_cross_q.shape, half),
             ),
             in_specs=[hbm] * 6 + [vmem] * 3,
-            out_specs=(hbm, hbm),
+            out_specs=(vmem, hbm),
             scratch_shapes=[
                 pltpu.VMEM((video_count, 3, video_all, HEAD), half),
-                pltpu.VMEM((video_count, video_all, HEAD), half),
-                pltpu.VMEM((video_count, 2, audio_all, HEAD), half),
+                pltpu.VMEM((cross_count, near * video_local, HEAD), half),
+                pltpu.VMEM((cross_count, 2, audio_all, HEAD), half),
                 pltpu.VMEM((audio_count, 3, audio_all, HEAD), half),
                 pltpu.VMEM((audio_count, audio_all, HEAD), half),
                 pltpu.VMEM((audio_count, 2, video_all, HEAD), half),
                 pltpu.VMEM((video_count, video_all, HEAD), half),
+                pltpu.VMEM((cross_count, near * video_local, HEAD), half),
                 pltpu.VMEM((audio_count, audio_all, HEAD), half),
-                pltpu.SemaphoreType.DMA((video_count, 3)),
+                pltpu.VMEM(video_cross_q.shape, half),
+                pltpu.VMEM(video_cross_q.shape, half),
+                pltpu.SemaphoreType.DMA((video_count,)),
+                pltpu.SemaphoreType.DMA((cross_count, 2)),
                 pltpu.SemaphoreType.DMA((audio_count, 3)),
-                pltpu.SemaphoreType.DMA((8,)),
-                pltpu.SemaphoreType.DMA((2,)),
+                pltpu.SemaphoreType.DMA((9,)),
+                pltpu.SemaphoreType.DMA((3,)),
             ],
             compiler_params=pltpu.CompilerParams(
-                collective_id=0, has_side_effects=True, vmem_limit_bytes=48 * 2**20
+                collective_id=0, has_side_effects=True, vmem_limit_bytes=52 * 2**20
             ),
         )(
-            by_items(video_qkv, HV),
+            kinds_first(video_qkv),
             video_cross_q,
-            by_items(audio_kv_v, HV),
-            by_items(audio_qkv, HA),
+            kinds_first(audio_kv_v),
+            kinds_first(audio_qkv),
             audio_cross_q,
-            by_items(video_kv_a, HA),
-            video_gates.reshape(branches * HV, 1, HEAD),
+            kinds_first(video_kv_a),
+            video_gates.reshape(branches, 1, -1),
             audio_gates.reshape(branches * HA, 1, HEAD),
             bias.reshape(branches, 1, audio_all),
         )

time: 283 us -> 263 us (0.929)
  local copies, waits for them, and re-layouts: 18.9 us -> 8 us
  Pallas kernels: 260 us -> 251 us
    reshape x7 -> x1, local copies, waits for them, and re-layouts: 17.1 us -> 0.02 us  [on_device(): video_gates.reshape(branches, 1, -1)]
    pallas_call x1, Pallas kernels: 260 us -> 251 us  [on_device(): pl.pallas_call(functools.partial(block_kernel, n, video_count, cross_coun...]
    unnamed x8 -> x12, local copies, waits for them, and re-layouts: 1.86 us -> 7.95 us
where the time goes in v2:
time: 263 us; the launch traced here: 262 us
  Pallas kernels  251 us (95%)
  local copies, waits for them, and re-layouts  8 us (3%)
    pallas_call x1, Pallas kernels, on_device(): pl.pallas_call(functools.partial(block_kernel, n, video_count, cross_coun...  251 us
    unnamed x12, local copies, waits for them, and re-layouts  7.95 us

profile of v2, /device:TPU:0, one launch (start us, length us, event | category | flops | bytes accessed | tf_op | source)
XLA Modules:
  0.0 262.5 jit_solution(6859771742655578392)
XLA Ops:
  0.6 0.0 copy-start
  0.6 0.0 copy-start.3
  0.7 0.8 compare_select_fusion.bias
  1.5 1.0 fusion
  2.5 0.0 copy-done
  2.5 0.9 fusion.1
  3.5 2.8 %copy.17 = bf16[2,32,2,4096]{3,1,2,0:T(8,128)(2,1)} copy(bf16[2,32,2,4096]{3,2,1,0:T(2,128)(2,1)} %param.12) | data formatting | bytes 2097152 | tf_op args[2]
  6.3 0.0 copy-done.3
  6.3 0.0 copy-start.1
  6.3 0.0 copy-start.2
  6.3 1.8 copy.16
  8.0 0.0 copy-done.1
  8.0 0.0 copy-done.2
  8.0 251.1 %shard_map.113 = (bf16[2,96,4096]{2,1,0:T(8,128)(2,1)}, bf16[2,32,2048]{2,1,0:T(8,128)(2,1)S(1)}) custom-call(bf16[2,3,96,4096]{3,2,1,0:T(8,128)(2,1)} %bitcast.12, bf16[2,96,4096]{2,1,0:T(8,128)(2,1)} %video_q.1, bf16[2,2,32,4096]{3,2,1,0:T(8,128)(2,1)} %bitcast.13, bf16[2,3,32,2048]{3,2,1,0:T(8,128)(2,1)S(1)} %bitcast.10, ...), custom_call_target="tpu_custom_call" | custom-call | tf_op jit(solution)/shard_map/pallas_call | solution.py:356
  259.1 2.7 %copy.20 = bf16[2,96,4096]{2,1,0:T(8,128)(2,1)} copy(bf16[2,96,4096]{2,1,0:T(8,128)(2,1)} %get-tuple-element.4) | data formatting | bytes 3145728
  261.8 0.7 copy.21
  (2 shorter events, 0.1 us)
Async XLA Ops:
  0.6 1.9 copy-start
  0.6 5.6 %copy-start.3 = (bf16[2,96,2,2048]{3,2,1,0:T(2,128)(2,1)S(1)}, bf16[2,96,2,2048]{3,2,1,0:T(2,128)(2,1)}, u32[]{:S(2)}) copy-start(bf16[2,96,2,2048]{3,2,1,0:T(2,128)(2,1)} %param.15) | copy-start | bytes 4718596
  6.3 1.8 copy-start.1
  6.3 1.8 copy-start.2

commit v3 on v2

--- a/solution.py
+++ b/solution.py
@@ -26,7 +26,7 @@
     result = jnp.dot(
         weights.astype(jnp.bfloat16), value_rows, preferred_element_type=jnp.float32
     )
-    return (result / total).astype(jnp.bfloat16).astype(jnp.float32)
+    return result / total, row_max + jnp.log(total)
 
 
 def block_kernel(
@@ -34,6 +34,7 @@
     video_count,
     cross_count,
     audio_count,
+    across_count,
     video_block,
     audio_block,
     video_qkv,
@@ -56,11 +57,18 @@
     video_res,
     cross_res,
     audio_res,
+    across_res,
+    level_res,
     own_home,
     cross_home,
+    audio_home,
+    across_home,
+    level_home,
+    share_mat,
     video_sems,
     cross_sems,
     audio_sems,
+    across_sems,
     send_sems,
     back_sems,
 ):
@@ -126,17 +134,27 @@
             (
                 audio_qkv.at[branch, :, :, columns(head)],
                 audio_qkv_in.at[slot, :, audio_rows],
-                audio_sems.at[slot, 0],
-            ),
+                audio_sems.at[slot],
+            ),
+        )
+
+    def across_q_parts(item, slot):
+        branch, head = item // HA, lax.rem(item, HA)
+        return (
             (
                 audio_q.at[branch, :, columns(head)],
                 audio_q_in.at[slot, audio_rows],
-                audio_sems.at[slot, 1],
-            ),
+                across_sems.at[slot, 0],
+            ),
+        )
+
+    def across_kv_parts(item, slot):
+        branch, head = item // HA, lax.rem(item, HA)
+        return (
             (
                 video_kv.at[branch, :, :, columns(head)],
-                video_kv_in.at[slot, :, video_rows],
-                audio_sems.at[slot, 2],
+                video_kv_in.at[slot, :, half_rows],
+                across_sems.at[slot, 1],
             ),
         )
 
@@ -162,6 +180,7 @@
             pltpu.make_async_copy(source, target, sem).start()
 
     per_video = cross_count // video_count
+    per_audio = across_count // audio_count
 
     def send_video(slot, carry):
         send(video_parts, video_count, slot, 0, 0, n, n)
@@ -176,6 +195,13 @@
 
     def send_audio(slot, carry):
         send(audio_parts, audio_count, slot, 3, 0, n, n)
+
+        def send_across(j, inner):
+            send(across_q_parts, across_count, slot * per_audio + j, 4, 0, n, near)
+            send(across_kv_parts, across_count, slot * per_audio + j, 5, half_first, near, near)
+            return inner
+
+        lax.fori_loop(0, per_audio, send_across, 0)
         return carry
 
     lax.fori_loop(0, video_count, send_video, 0)
@@ -217,7 +243,7 @@
 
         def rows(i, inner):
             here = pl.ds(pl.multiple_of(i * block, block), block)
-            own = attend(
+            own, _ = attend(
                 video_qkv_in[slot, 0, here], video_qkv_in[slot, 1], video_qkv_in[slot, 2], None
             )
             video_res[slot, here] = own.astype(jnp.bfloat16)
@@ -245,7 +271,7 @@
 
         def rows(i, inner):
             here = pl.ds(pl.multiple_of(i * block, block), block)
-            cross = attend(
+            cross, _ = attend(
                 video_q_in[slot, here], audio_kv_in[slot, 0], audio_kv_in[slot, 1], bias[branch]
             )
             cross_res[slot, here] = cross.astype(jnp.bfloat16)
@@ -260,31 +286,77 @@
     def audio_item(slot, carry):
         item = me * audio_count + slot
         branch, head = item // HA, lax.rem(item, HA)
-        settle(audio_qkv_in.at[slot], audio_sems.at[slot, 0])
-        settle(audio_q_in.at[slot], audio_sems.at[slot, 1])
-        settle(video_kv_in.at[slot], audio_sems.at[slot, 2])
+        settle(audio_qkv_in.at[slot], audio_sems.at[slot])
         block = audio_block * audio_local
 
         def rows(i, inner):
             here = pl.ds(pl.multiple_of(i * block, block), block)
-            own = attend(
+            own, _ = attend(
                 audio_qkv_in[slot, 0, here],
                 audio_qkv_in[slot, 1],
                 audio_qkv_in[slot, 2],
                 bias[branch],
             )
-            cross = attend(
+            audio_res[slot, here] = own.astype(jnp.bfloat16)
+            give_back(
+                audio_res, slot, audio_home, branch, head, audio_local, 0, i * audio_block,
+                audio_block, 1,
+            )
+            return inner
+
+        lax.fori_loop(0, n // audio_block, rows, 0)
+
+        def across(j, inner):
+            across_item(slot * per_audio + j)
+            return inner
+
+        lax.fori_loop(0, per_audio, across, 0)
+        return carry
+
+    my_half = me // near
+
+    def across_item(slot):
+        item = place_in_half * across_count + slot
+        branch, head = item // HA, lax.rem(item, HA)
+        settle(audio_q_in.at[slot], across_sems.at[slot, 0])
+        settle(video_kv_in.at[slot], across_sems.at[slot, 1])
+        block = audio_block * audio_local
+
+        def rows(i, inner):
+            here = pl.ds(pl.multiple_of(i * block, block), block)
+            part, level = attend(
                 audio_q_in[slot, here], video_kv_in[slot, 0], video_kv_in[slot, 1], None
             )
-            audio_res[slot, here] = (own + audio_gates[item] * cross).astype(jnp.bfloat16)
+            across_res[slot, here] = part.astype(jnp.bfloat16)
+            for c in range(block // HEAD):
+                column = jnp.broadcast_to(level[c * HEAD : (c + 1) * HEAD], (HEAD, HEAD))
+                level_res[slot, i * (block // HEAD) + c] = jnp.transpose(column)[0:1]
             give_back(
-                audio_res, slot, audio_out, branch, head, audio_local, 0, i * audio_block,
-                audio_block, 1,
+                across_res, slot, across_home.at[my_half], branch, head, audio_local, 0,
+                i * audio_block, audio_block, 3,
             )
             return inner
 
         lax.fori_loop(0, n // audio_block, rows, 0)
-        return carry
+
+        def levels(k, inner):
+            peer = lax.rem(me + k, n)
+            pltpu.make_async_remote_copy(
+                src_ref=level_res.at[slot, (peer * audio_local) // HEAD],
+                dst_ref=level_home.at[my_half * (audio_home.shape[0] * HA) + item],
+                send_sem=send_sems.at[10],
+                recv_sem=back_sems.at[4],
+                device_id=(group, peer),
+                device_id_type=MESH,
+            ).start()
+            return inner
+
+        lax.fori_loop(1, n, levels, 0)
+        pltpu.make_async_copy(
+            level_res.at[slot, (me * audio_local) // HEAD],
+            level_home.at[my_half * (audio_home.shape[0] * HA) + item],
+            back_sems.at[4],
+        ).start()
 
     lax.fori_loop(0, video_count, video_item, 0)
     lax.fori_loop(0, audio_count, audio_item, 0)
@@ -304,6 +376,26 @@
 
     lax.fori_loop(0, video_out.shape[2] // width, combine, 0)
 
+    settle(audio_home, back_sems.at[1])
+    settle(across_home, back_sems.at[3])
+    settle(level_home, back_sems.at[4])
+    items = level_home.shape[0] // 2
+    low, high = level_home[:items, 0], level_home[items:, 0]
+    for place, gap in enumerate((high - low, low - high)):
+        share_mat[place] = jnp.transpose(1.0 / (1.0 + jnp.exp(gap)))
+    mine = pl.ds(pl.multiple_of(lax.rem(me * audio_local, HEAD), audio_local), audio_local)
+    low_share, high_share = share_mat[0, mine], share_mat[1, mine]
+    for item in range(low_share.shape[1]):
+        branch, head = item // HA, item % HA
+        here = slice(head * HEAD, (head + 1) * HEAD)
+        across = (
+            low_share[:, item : item + 1] * across_home[0, branch, :, here].astype(jnp.float32)
+            + high_share[:, item : item + 1] * across_home[1, branch, :, here].astype(jnp.float32)
+        )
+        audio_out[branch, :, here] = (
+            audio_home[branch, :, here].astype(jnp.float32) + audio_gates[item] * across
+        ).astype(jnp.bfloat16)
+
     far_video = pl.ds(0, (n - 1) * video_local)
     far_audio = pl.ds(0, (n - 1) * audio_local)
     far_half = pl.ds(0, (near - 1) * video_local)
@@ -312,11 +404,12 @@
     settle(audio_kv_in.at[:, :, far_audio], send_sems.at[2])
     settle(audio_qkv_in.at[:, :, far_audio], send_sems.at[3])
     settle(audio_q_in.at[:, far_audio], send_sems.at[4])
-    settle(video_kv_in.at[:, :, far_video], send_sems.at[5])
+    settle(video_kv_in.at[:, :, far_half], send_sems.at[5])
     settle(video_res.at[:, far_video], send_sems.at[6])
     settle(audio_res.at[:, far_audio], send_sems.at[7])
     settle(cross_res.at[:, far_half], send_sems.at[8])
-    settle(audio_out, back_sems.at[1])
+    settle(across_res.at[:, far_audio], send_sems.at[9])
+    settle(level_home.at[pl.ds(0, across_count * (n - 1))], send_sems.at[10])
 
 
 def kinds_first(source):
@@ -341,7 +434,7 @@
     video_all, audio_all = video_local * n, audio_local * n
     video_count, audio_count = branches * HV // n, branches * HA // n
     near = n // 2
-    cross_count = branches * HV // near
+    cross_count, across_count = branches * HV // near, branches * HA // near
     positions = jnp.arange(audio_all, dtype=jnp.int32)
     bias = jnp.where(positions[None, :] < audio_valid[:, None], 0.0, -jnp.inf).astype(jnp.float32)
     chosen = (branch_prompt[:, None] == jnp.arange(PROMPTS, dtype=jnp.int32)[None, :]).astype(
@@ -355,31 +448,38 @@
     return tuple(
         pl.pallas_call(
             functools.partial(
-                block_kernel, n, video_count, cross_count, audio_count, min(4, near), min(8, n)
+                block_kernel, n, video_count, cross_count, audio_count, across_count, min(4, near), min(8, n)
             ),
             out_shape=(
                 jax.ShapeDtypeStruct(video_cross_q.shape, half),
                 jax.ShapeDtypeStruct(audio_cross_q.shape, half),
             ),
             in_specs=[hbm] * 6 + [vmem] * 3,
-            out_specs=(vmem, hbm),
+            out_specs=(vmem, vmem),
             scratch_shapes=[
                 pltpu.VMEM((video_count, 3, video_all, HEAD), half),
                 pltpu.VMEM((cross_count, near * video_local, HEAD), half),
                 pltpu.VMEM((cross_count, 2, audio_all, HEAD), half),
                 pltpu.VMEM((audio_count, 3, audio_all, HEAD), half),
-                pltpu.VMEM((audio_count, audio_all, HEAD), half),
-                pltpu.VMEM((audio_count, 2, video_all, HEAD), half),
+                pltpu.VMEM((across_count, audio_all, HEAD), half),
+                pltpu.VMEM((across_count, 2, near * video_local, HEAD), half),
                 pltpu.VMEM((video_count, video_all, HEAD), half),
                 pltpu.VMEM((cross_count, near * video_local, HEAD), half),
                 pltpu.VMEM((audio_count, audio_all, HEAD), half),
+                pltpu.VMEM((across_count, audio_all, HEAD), half),
+                pltpu.VMEM((across_count, audio_all // HEAD, 1, HEAD), jnp.float32),
                 pltpu.VMEM(video_cross_q.shape, half),
                 pltpu.VMEM(video_cross_q.shape, half),
+                pltpu.VMEM(audio_cross_q.shape, half),
+                pltpu.VMEM((2,) + audio_cross_q.shape, half),
+                pltpu.VMEM((2 * branches * HA, 1, HEAD), jnp.float32),
+                pltpu.VMEM((2, HEAD, branches * HA), jnp.float32),
                 pltpu.SemaphoreType.DMA((video_count,)),
                 pltpu.SemaphoreType.DMA((cross_count, 2)),
-                pltpu.SemaphoreType.DMA((audio_count, 3)),
-                pltpu.SemaphoreType.DMA((9,)),
-                pltpu.SemaphoreType.DMA((3,)),
+                pltpu.SemaphoreType.DMA((audio_count,)),
+                pltpu.SemaphoreType.DMA((across_count, 2)),
+                pltpu.SemaphoreType.DMA((11,)),
+                pltpu.SemaphoreType.DMA((5,)),
             ],
             compiler_params=pltpu.CompilerParams(
                 collective_id=0, has_side_effects=True, vmem_limit_bytes=52 * 2**20

time: 263 us -> 249 us (0.947)
  Pallas kernels: 251 us -> 237 us
    pallas_call x1, Pallas kernels: 251 us -> 237 us  [on_device(): pl.pallas_call(functools.partial(block_kernel, n, video_count, cross_coun...]
where the time goes in v3:
time: 249 us
  Pallas kernels  237 us (95%)
  local copies, waits for them, and re-layouts  8 us (3%)
    pallas_call x1, Pallas kernels, on_device(): pl.pallas_call(functools.partial(block_kernel, n, video_count, cross_coun...  237 us
    unnamed x12, local copies, waits for them, and re-layouts  7.95 us

profile of v3, /device:TPU:0, one launch (start us, length us, event | category | flops | bytes accessed | tf_op | source)
XLA Modules:
  0.0 248.9 jit_solution(17812462474105235425)
XLA Ops:
  0.6 0.0 copy-start
  0.6 0.0 copy-start.3
  0.7 0.8 compare_select_fusion.bias
  1.5 1.0 fusion
  2.5 0.0 copy-done
  2.5 0.9 fusion.1
  3.5 2.8 %copy.17 = bf16[2,32,2,4096]{3,1,2,0:T(8,128)(2,1)} copy(bf16[2,32,2,4096]{3,2,1,0:T(2,128)(2,1)} %param.12) | data formatting | bytes 2097152 | tf_op args[2]
  6.3 0.0 copy-done.3
  6.3 0.0 copy-start.1
  6.3 0.0 copy-start.2
  6.3 1.8 copy.16
  8.0 0.0 copy-done.1
  8.0 0.0 copy-done.2
  8.0 237.5 %shard_map.113 = (bf16[2,96,4096]{2,1,0:T(8,128)(2,1)}, bf16[2,32,2048]{2,1,0:T(8,128)(2,1)S(1)}) custom-call(bf16[2,3,96,4096]{3,2,1,0:T(8,128)(2,1)} %bitcast.12, bf16[2,96,4096]{2,1,0:T(8,128)(2,1)} %video_q.1, bf16[2,2,32,4096]{3,2,1,0:T(8,128)(2,1)} %bitcast.13, bf16[2,3,32,2048]{3,2,1,0:T(8,128)(2,1)S(1)} %bitcast.10, ...), custom_call_target="tpu_custom_call" | custom-call | tf_op jit(solution)/shard_map/pallas_call | solution.py:449
  245.5 2.7 %copy.20 = bf16[2,96,4096]{2,1,0:T(8,128)(2,1)} copy(bf16[2,96,4096]{2,1,0:T(8,128)(2,1)} %get-tuple-element.4) | data formatting | bytes 3145728
  248.2 0.7 copy.21
  (2 shorter events, 0.1 us)
Async XLA Ops:
  0.6 1.9 copy-start
  0.6 5.6 %copy-start.3 = (bf16[2,96,2,2048]{3,2,1,0:T(2,128)(2,1)S(1)}, bf16[2,96,2,2048]{3,2,1,0:T(2,128)(2,1)}, u32[]{:S(2)}) copy-start(bf16[2,96,2,2048]{3,2,1,0:T(2,128)(2,1)} %param.15) | copy-start | bytes 4718596
  6.3 1.8 copy-start.1
  6.3 1.8 copy-start.2

commit v4 on v3

--- a/solution.py
+++ b/solution.py
@@ -179,15 +179,19 @@
         for source, target, sem in items_of(me):
             pltpu.make_async_copy(source, target, sem).start()
 
-    per_video = cross_count // video_count
+    per_video = cross_count // (video_count - audio_count)
     per_audio = across_count // audio_count
 
     def send_video(slot, carry):
         send(video_parts, video_count, slot, 0, 0, n, n)
+        return carry
+
+    def send_crosses(slot, carry):
+        first = (slot - audio_count) * per_video
 
         def send_cross(j, inner):
-            send(cross_q_parts, cross_count, slot * per_video + j, 1, half_first, near, near)
-            send(cross_kv_parts, cross_count, slot * per_video + j, 2, 0, n, near)
+            send(cross_kv_parts, cross_count, first + j, 2, 0, n, near)
+            send(cross_q_parts, cross_count, first + j, 1, half_first, near, near)
             return inner
 
         lax.fori_loop(0, per_video, send_cross, 0)
@@ -204,8 +208,19 @@
         lax.fori_loop(0, per_audio, send_across, 0)
         return carry
 
-    lax.fori_loop(0, video_count, send_video, 0)
-    lax.fori_loop(0, audio_count, send_audio, 0)
+    def early(slot, carry, video, other):
+        video(slot, carry)
+        return other(slot, carry)
+
+    lax.fori_loop(
+        0, audio_count, functools.partial(early, video=send_video, other=send_audio), 0
+    )
+    lax.fori_loop(
+        audio_count,
+        video_count,
+        functools.partial(early, video=send_video, other=send_crosses),
+        0,
+    )
 
     def settle(ref, sem):
         pltpu.make_async_copy(ref, ref, sem).wait()
@@ -254,9 +269,11 @@
             return inner
 
         lax.fori_loop(0, n // video_block, rows, 0)
-
+        return carry
+
+    def cross_items(slot, carry):
         def cross(j, inner):
-            cross_item(slot * per_video + j)
+            cross_item((slot - audio_count) * per_video + j)
             return inner
 
         lax.fori_loop(0, per_video, cross, 0)
@@ -358,23 +375,15 @@
             back_sems.at[4],
         ).start()
 
-    lax.fori_loop(0, video_count, video_item, 0)
-    lax.fori_loop(0, audio_count, audio_item, 0)
-
-    settle(own_home, back_sems.at[0])
-    settle(cross_home, back_sems.at[2])
-    width = 512
-
-    def combine(i, carry):
-        here = pl.ds(pl.multiple_of(i * width, width), width)
-        for branch in range(own_home.shape[0]):
-            video_out[branch, :, here] = (
-                own_home[branch, :, here].astype(jnp.float32)
-                + video_gates[branch, :, here] * cross_home[branch, :, here].astype(jnp.float32)
-            ).astype(jnp.bfloat16)
-        return carry
-
-    lax.fori_loop(0, video_out.shape[2] // width, combine, 0)
+    lax.fori_loop(
+        0, audio_count, functools.partial(early, video=video_item, other=audio_item), 0
+    )
+    lax.fori_loop(
+        audio_count,
+        video_count,
+        functools.partial(early, video=video_item, other=cross_items),
+        0,
+    )
 
     settle(audio_home, back_sems.at[1])
     settle(across_home, back_sems.at[3])
@@ -395,6 +404,21 @@
         audio_out[branch, :, here] = (
             audio_home[branch, :, here].astype(jnp.float32) + audio_gates[item] * across
         ).astype(jnp.bfloat16)
+
+    settle(own_home, back_sems.at[0])
+    settle(cross_home, back_sems.at[2])
+    width = 512
+
+    def combine(i, carry):
+        here = pl.ds(pl.multiple_of(i * width, width), width)
+        for branch in range(own_home.shape[0]):
+            video_out[branch, :, here] = (
+                own_home[branch, :, here].astype(jnp.float32)
+                + video_gates[branch, :, here] * cross_home[branch, :, here].astype(jnp.float32)
+            ).astype(jnp.bfloat16)
+        return carry
+
+    lax.fori_loop(0, video_out.shape[2] // width, combine, 0)
 
     far_video = pl.ds(0, (n - 1) * video_local)
     far_audio = pl.ds(0, (n - 1) * audio_local)

time: 249 us -> 247 us (level)
  Pallas kernels: 237 us -> 234 us
    pallas_call x1, Pallas kernels: 237 us -> 234 us  [on_device(): pl.pallas_call(functools.partial(block_kernel, n, video_count, cross_coun...]
where the time goes in v4:
time: 247 us; the launch traced here: 245 us
  Pallas kernels  234 us (95%)
  local copies, waits for them, and re-layouts  8 us (3%)
    pallas_call x1, Pallas kernels, on_device(): pl.pallas_call(functools.partial(block_kernel, n, video_count, cross_coun...  234 us
    unnamed x12, local copies, waits for them, and re-layouts  7.95 us

profile of v4, /device:TPU:0, one launch (start us, length us, event | category | flops | bytes accessed | tf_op | source)
XLA Modules:
  0.0 245.4 jit_solution(17952562872891234920)
XLA Ops:
  0.6 0.0 copy-start
  0.6 0.0 copy-start.3
  0.7 0.8 compare_select_fusion.bias
  1.5 1.0 fusion
  2.5 0.0 copy-done
  2.5 0.9 fusion.1
  3.5 2.8 %copy.17 = bf16[2,32,2,4096]{3,1,2,0:T(8,128)(2,1)} copy(bf16[2,32,2,4096]{3,2,1,0:T(2,128)(2,1)} %param.12) | data formatting | bytes 2097152 | tf_op args[2]
  6.3 0.0 copy-done.3
  6.3 0.0 copy-start.1
  6.3 0.0 copy-start.2
  6.3 1.8 copy.16
  8.0 0.0 copy-done.1
  8.0 0.0 copy-done.2
  8.0 233.9 %shard_map.113 = (bf16[2,96,4096]{2,1,0:T(8,128)(2,1)}, bf16[2,32,2048]{2,1,0:T(8,128)(2,1)S(1)}) custom-call(bf16[2,3,96,4096]{3,2,1,0:T(8,128)(2,1)} %bitcast.12, bf16[2,96,4096]{2,1,0:T(8,128)(2,1)} %video_q.1, bf16[2,2,32,4096]{3,2,1,0:T(8,128)(2,1)} %bitcast.13, bf16[2,3,32,2048]{3,2,1,0:T(8,128)(2,1)S(1)} %bitcast.10, ...), custom_call_target="tpu_custom_call" | custom-call | tf_op jit(solution)/shard_map/pallas_call | solution.py:473
  242.0 2.7 %copy.20 = bf16[2,96,4096]{2,1,0:T(8,128)(2,1)} copy(bf16[2,96,4096]{2,1,0:T(8,128)(2,1)} %get-tuple-element.4) | data formatting | bytes 3145728
  244.7 0.7 copy.21
  (2 shorter events, 0.1 us)
Async XLA Ops:
  0.6 1.9 copy-start
  0.6 5.6 %copy-start.3 = (bf16[2,96,2,2048]{3,2,1,0:T(2,128)(2,1)S(1)}, bf16[2,96,2,2048]{3,2,1,0:T(2,128)(2,1)}, u32[]{:S(2)}) copy-start(bf16[2,96,2,2048]{3,2,1,0:T(2,128)(2,1)} %param.15) | copy-start | bytes 4718596
  6.3 1.8 copy-start.1
  6.3 1.8 copy-start.2

commit v5 on v4

--- a/solution.py
+++ b/solution.py
@@ -43,9 +43,10 @@
     audio_qkv,
     audio_q,
     video_kv,
-    video_gates,
-    audio_gates,
-    bias,
+    video_gate,
+    audio_gate,
+    audio_valid,
+    branch_prompt,
     video_out,
     audio_out,
     video_qkv_in,
@@ -163,7 +164,8 @@
             return parts(lax.rem(peer, ring) * count + slot, slot)
 
         def to_peer(k, carry):
-            peer = first + lax.rem(me - first + k, span)
+            step = k // 2 + lax.rem(k, 2) * (span // 2)
+            peer = first + lax.rem(me - first + step, span)
             for place, (source, target, sem) in enumerate(items_of(peer)):
                 pltpu.make_async_remote_copy(
                     src_ref=source,
@@ -222,6 +224,17 @@
         0,
     )
 
+    def mask(branch):
+        positions = lax.broadcasted_iota(jnp.int32, (1, audio_kv_in.shape[2]), 1)
+        return jnp.where(positions < audio_valid[branch], 0.0, -jnp.inf)
+
+    def gate_of(gates, branch, here):
+        return sum(
+            (branch_prompt[branch] == p).astype(jnp.int32).astype(jnp.float32)
+            * gates[p : p + 1, here]
+            for p in range(PROMPTS)
+        )
+
     def settle(ref, sem):
         pltpu.make_async_copy(ref, ref, sem).wait()
 
@@ -289,7 +302,7 @@
         def rows(i, inner):
             here = pl.ds(pl.multiple_of(i * block, block), block)
             cross, _ = attend(
-                video_q_in[slot, here], audio_kv_in[slot, 0], audio_kv_in[slot, 1], bias[branch]
+                video_q_in[slot, here], audio_kv_in[slot, 0], audio_kv_in[slot, 1], mask(branch)
             )
             cross_res[slot, here] = cross.astype(jnp.bfloat16)
             give_back(
@@ -312,7 +325,7 @@
                 audio_qkv_in[slot, 0, here],
                 audio_qkv_in[slot, 1],
                 audio_qkv_in[slot, 2],
-                bias[branch],
+                mask(branch),
             )
             audio_res[slot, here] = own.astype(jnp.bfloat16)
             give_back(
@@ -402,7 +415,7 @@
             + high_share[:, item : item + 1] * across_home[1, branch, :, here].astype(jnp.float32)
         )
         audio_out[branch, :, here] = (
-            audio_home[branch, :, here].astype(jnp.float32) + audio_gates[item] * across
+            audio_home[branch, :, here].astype(jnp.float32) + gate_of(audio_gate, branch, here) * across
         ).astype(jnp.bfloat16)
 
     settle(own_home, back_sems.at[0])
@@ -414,7 +427,7 @@
         for branch in range(own_home.shape[0]):
             video_out[branch, :, here] = (
                 own_home[branch, :, here].astype(jnp.float32)
-                + video_gates[branch, :, here] * cross_home[branch, :, here].astype(jnp.float32)
+                + gate_of(video_gate, branch, here) * cross_home[branch, :, here].astype(jnp.float32)
             ).astype(jnp.bfloat16)
         return carry
 
@@ -459,15 +472,9 @@
     video_count, audio_count = branches * HV // n, branches * HA // n
     near = n // 2
     cross_count, across_count = branches * HV // near, branches * HA // near
-    positions = jnp.arange(audio_all, dtype=jnp.int32)
-    bias = jnp.where(positions[None, :] < audio_valid[:, None], 0.0, -jnp.inf).astype(jnp.float32)
-    chosen = (branch_prompt[:, None] == jnp.arange(PROMPTS, dtype=jnp.int32)[None, :]).astype(
-        jnp.float32
-    )
-    video_gates = jnp.dot(chosen, video_gate, precision=lax.Precision.HIGHEST)
-    audio_gates = jnp.dot(chosen, audio_gate, precision=lax.Precision.HIGHEST)
     hbm = pl.BlockSpec(memory_space=pl.ANY)
     vmem = pl.BlockSpec(memory_space=pltpu.VMEM)
+    smem = pl.BlockSpec(memory_space=pltpu.SMEM)
     half = jnp.bfloat16
     return tuple(
         pl.pallas_call(
@@ -478,7 +485,7 @@
                 jax.ShapeDtypeStruct(video_cross_q.shape, half),
                 jax.ShapeDtypeStruct(audio_cross_q.shape, half),
             ),
-            in_specs=[hbm] * 6 + [vmem] * 3,
+            in_specs=[hbm] * 6 + [vmem] * 2 + [smem] * 2,
             out_specs=(vmem, vmem),
             scratch_shapes=[
                 pltpu.VMEM((video_count, 3, video_all, HEAD), half),
@@ -515,9 +522,10 @@
             kinds_first(audio_qkv),
             audio_cross_q,
             kinds_first(video_kv_a),
-            video_gates.reshape(branches, 1, -1),
-            audio_gates.reshape(branches * HA, 1, HEAD),
-            bias.reshape(branches, 1, audio_all),
+            video_gate,
+            audio_gate,
+            audio_valid,
+            branch_prompt,
         )
     )
 

time: 247 us -> 243 us (0.984)
    unnamed x12 -> x18, local copies, waits for them, and re-layouts: 7.95 us -> 8.1 us
where the time goes in v5:
time: 243 us; the launch traced here: 242 us
  Pallas kernels  233 us (96%)
  local copies, waits for them, and re-layouts  8.1 us (3%)
    pallas_call x1, Pallas kernels, on_device(): pl.pallas_call(functools.partial(block_kernel, n, video_count, cross_coun...  233 us
    unnamed x18, local copies, waits for them, and re-layouts  8.1 us

profile of v5, /device:TPU:0, one launch (start us, length us, event | category | flops | bytes accessed | tf_op | source)
XLA Modules:
  0.0 241.8 jit_solution(15785919165196171971)
XLA Ops:
  0.6 0.0 copy-start.6
  0.6 2.9 %copy.17 = bf16[2,32,2,4096]{3,1,2,0:T(8,128)(2,1)} copy(bf16[2,32,2,4096]{3,2,1,0:T(2,128)(2,1)} %param.12) | data formatting | bytes 2097152 | tf_op args[2]
  3.5 0.0 copy-done.6
  3.5 0.0 copy-start
  3.5 0.0 copy-start.1
  3.5 0.0 copy-start.2
  3.6 0.0 copy-start.3
  3.6 0.0 copy-start.4
  3.6 0.0 copy-start.5
  3.6 1.8 copy.16
  5.4 0.0 copy-done
  5.4 0.0 copy-done.1
  5.4 0.0 copy-done.2
  5.4 0.0 copy-done.3
  5.4 0.0 copy-done.4
  5.4 0.0 copy-done.5
  5.4 233.0 %shard_map.113 = (bf16[2,96,4096]{2,1,0:T(8,128)(2,1)}, bf16[2,32,2048]{2,1,0:T(8,128)(2,1)S(1)}) custom-call(bf16[2,3,96,4096]{3,2,1,0:T(8,128)(2,1)} %bitcast.10, bf16[2,96,4096]{2,1,0:T(8,128)(2,1)} %video_q.1, bf16[2,2,32,4096]{3,2,1,0:T(8,128)(2,1)} %bitcast.11, bf16[2,3,32,2048]{3,2,1,0:T(8,128)(2,1)S(1)} %bitcast.8, ...), custom_call_target="tpu_custom_call" | custom-call | tf_op jit(solution)/shard_map/pallas_call | solution.py:480
  238.4 2.7 %copy.20 = bf16[2,96,4096]{2,1,0:T(8,128)(2,1)} copy(bf16[2,96,4096]{2,1,0:T(8,128)(2,1)} %get-tuple-element.4) | data formatting | bytes 3145728
  241.1 0.7 copy.21
Async XLA Ops:
  0.6 2.9 %copy-start.6 = (bf16[2,96,2,2048]{3,2,1,0:T(2,128)(2,1)S(1)}, bf16[2,96,2,2048]{3,2,1,0:T(2,128)(2,1)}, u32[]{:S(2)}) copy-start(bf16[2,96,2,2048]{3,2,1,0:T(2,128)(2,1)} %param.15) | copy-start | bytes 4718596
  3.5 1.8 copy-start
  3.5 1.8 copy-start.1
  3.5 1.8 copy-start.2
  3.6 1.8 copy-start.3
  3.6 1.8 copy-start.4
  3.6 1.8 copy-start.5
